TPU v7x, 512 devices: a whole 4x8x8 slice. The times are simulated.
512 devices in a mesh: row: 16 (over x, z_lo), col: 32 (over y, z_hi, core).
Axes of the slice: x: 4, y: 8, z: 8 (z_hi: 2, z_lo: 4; z = z_hi * 4 + z_lo), core: 2. Of those that a mesh axis runs over, the one named last changes fastest.
Arguments:
- amplitudes: float32 [32, 96, 4, 128, 128], P('col', 'row'), may hold values from -6 to 6
- integrals: float32 [2, 2048, 16384], P(None, 'row', 'col'), may hold values from -0.25 to 0.25
- owner_column: int32 [2], replicated, may hold values from 0 to 31
- occ_irrep: int32 [96], replicated, may hold values from 0 to 7, as said below
- pair_irrep: int32 [2, 16], replicated, may hold values from 0 to 7, as said below
Outputs:
- ladder: float32 [12288, 16384], P('row', 'col')
Inputs may be any that keep to these rules, and one draw needn't show every extreme that they name: `occ_irrep`: every irrep 0 to 7 labels some occupied-pair tile. `pair_irrep`: in each section no irrep labels more than 4 of the 16 panel tiles, and some irrep labels exactly 4.
All inputs are finite; a program needn't handle non-finite values.
Results may differ from a plain program's by a relative error of at most 0.0001.
Values sent between devices are 32-bit elements; how exact they have to be, the bound alone decides.
A program may use at most 64 MiB of HBM per device.

v0:
```python
import jax
import jax.numpy as jnp
from jax import lax
from jax.sharding import PartitionSpec as P


def spread(value, axis, source):
    kept = jnp.where(lax.axis_index(axis) == source, value, 0).astype(value.dtype)
    return lax.psum(kept, axis)


def slot_tables(occ_labels, pair_labels, slot_count):
    matches = occ_labels[:, None] == pair_labels[None, :]
    order_rank = jnp.cumsum(matches.astype(jnp.int32), axis=1) - 1
    slot_ids = jnp.arange(slot_count, dtype=jnp.int32)
    chosen = matches[:, None, :] & (order_rank[:, None, :] == slot_ids[None, :, None])
    positions = jnp.arange(pair_labels.shape[0], dtype=jnp.int32)
    tile_index = jnp.sum(chosen.astype(jnp.int32) * positions[None, None, :], axis=2)
    valid_slot = jnp.any(chosen, axis=2)
    return (tile_index, valid_slot, chosen)


def on_device(amplitudes, integrals, owner_column, occ_irrep, pair_irrep):
    tiles_here = amplitudes.shape[1]
    slot_count = amplitudes.shape[2]
    tile_size = amplitudes.shape[3]
    section_count = integrals.shape[0]
    columns = integrals.shape[2]
    first_tile = lax.axis_index("row") * tiles_here
    occ_mine = lax.dynamic_slice_in_dim(occ_irrep, first_tile, tiles_here)

    def fetch_panel(which_section):
        return spread(amplitudes[0], "col", owner_column[which_section])

    tables = [
        slot_tables(occ_mine, pair_irrep[which_section], slot_count)
        for which_section in range(section_count)
    ]
    panels = [fetch_panel(which_section) for which_section in range(section_count)]
    section_rows = [
        lax.all_gather(integrals[which_section], "row", axis=0, tiled=True)
        for which_section in range(section_count)
    ]
    running = jnp.zeros((tiles_here, tile_size, columns), jnp.float32)
    for which_section in range(section_count):
        tile_index, valid_slot, chosen = tables[which_section]
        amp_panel = panels[which_section] * valid_slot[:, :, None, None].astype(jnp.float32)
        row_tiles = section_rows[which_section].reshape(-1, tile_size, columns)
        picked = jnp.take(row_tiles, tile_index, axis=0)
        running = running + jnp.einsum(
            "osij,osjv->oiv", amp_panel, picked, precision=lax.Precision.HIGHEST
        )
    return running.reshape(tiles_here * tile_size, columns)


def solution(mesh):
    return jax.shard_map(
        on_device,
        mesh=mesh,
        in_specs=(P("col", "row", None, None, None), P(None, "row", "col"), P(), P(), P()),
        out_specs=P("row", "col"),
        check_vma=False,
    )
```

profile of v0, /device:TPU:1, one launch (start us, length us, event | category | flops | bytes accessed | tf_op | source)
XLA Modules:
  0.0 477.0 jit_solution(14299060480379461248)
XLA Ops:
  7.4 0.0 copy-start.3
  7.4 0.0 copy-start.1
  7.4 0.0 all-gather.7.cloned.1.call-start
  7.4 2.0 fusion.24
  9.4 0.0 all-gather.7.cloned.1.call-update
  9.4 0.0 all-gather.5.cloned.1.call-start
  9.4 0.7 all-gather.5.cloned.1.call-update
  10.2 0.0 all-reduce.3.cloned.1.call-start
  10.2 0.0 copy-done.3
  10.2 0.6 fusion.25
  12.2 0.0 copy-done.1
  12.2 2.0 select_bitcast_fusion.1
  14.2 0.0 copy-start.5
  14.2 0.0 copy-start.4
  14.2 0.0 all-reduce.3.cloned.1.call-update
  14.3 0.6 copy-done.5
  14.9 0.1 dynamic_slice.3
  15.0 0.0 copy-done.4
  15.0 0.1 broadcast_compare_fusion.1
  15.1 0.2 reduce_window_sum.18
  15.2 0.2 select_reduce_fusion
  15.4 0.1 reshape.163
  15.5 0.2 fusion.18
  15.7 0.2 reduce_window_sum.17
  15.9 0.2 select_reduce_fusion.1
  16.1 0.1 reshape.159
  16.1 0.2 fusion.19
  16.4 133.2 %all-gather.7.cloned.1.call-done = f32[1,2048,512]{2,1,0:T(8,128)} async-done(((f32[1,128,512]{2,1,0:T(8,128)}), f32[1,2048,512]{2,1,0:T(8,128)}) %all-gather.7.cloned.1.call-update) | async-done | bytes 4194320 | tf_op jit(solution)/shard_map/all_gather | solution.py:41
  149.6 5.8 %gather_fusion.1 = f32[24,128,512]{2,1,0:T(8,128)} fusion(f32[16,128,512]{2,1,0:T(8,128)} %bitcast.23, s32[1024]{0:T(1024)S(1)} %pad_clamp_fusion), kind=kCustom, calls=%fused_computation.1.clone | custom fusion | bytes 12583008 | tf_op jit(solution)/shard_map/jit(_take)/gather | solution.py:49
  155.4 130.0 %all-gather.5.cloned.1.call-done = f32[1,2048,512]{2,1,0:T(8,128)} async-done(((f32[1,128,512]{2,1,0:T(8,128)}), f32[1,2048,512]{2,1,0:T(8,128)}) %all-gather.5.cloned.1.call-update) | async-done | bytes 4194320 | tf_op jit(solution)/shard_map/all_gather | solution.py:41
  285.4 5.8 %gather_fusion = f32[24,128,512]{2,1,0:T(8,128)} fusion(f32[16,128,512]{2,1,0:T(8,128)} %bitcast.24, s32[1024]{0:T(1024)S(1)} %pad_clamp_fusion.1), kind=kCustom, calls=%fused_computation.clone | custom fusion | bytes 12583008 | tf_op jit(solution)/shard_map/jit(_take)/gather | solution.py:49
  291.2 166.4 %all-reduce.3.cloned.1.call-done = (f32[6,4,128,128]{3,2,1,0:T(8,128)}, f32[6,4,128,128]{3,2,1,0:T(8,128)}) async-done(((f32[6,4,128,128]{3,2,1,0:T(8,128)}, f32[6,4,128,128]{3,2,1,0:T(8,128)}), (f32[6,4,128,128]{3,2,1,0:T(8,128)}, f32[6,4,128,128]{3,2,1,0:T(8,128)})) %all-reduce.3.cloned.1.call-update) | async-done | bytes 3145744 | tf_op jit(solution)/shard_map/psum | solution.py:9
  457.6 0.0 copy-start
  457.6 0.0 copy-start.2
  457.6 6.9 %fusion = f32[6,128,512,1]{2,1,3,0:T(8,128)S(1)} fusion(f32[6,4,128,512]{3,2,1,0:T(8,128)} %bitcast.21, pred[6,4]{1,0:T(8,128)(4,1)S(1)} %compare_and_fusion, f32[6,4,128,128]{3,2,1,0:T(8,128)} %get-tuple-element.6, f32[6,4]{1,0:T(8,128)S(1)} %convert_element_type.38), kind=kOutput, calls=%fused_computation.2 | convolution fusion | flops 2417885184 | bytes 9437304 | tf_op jit(solution)/shard_map/osij,osjv->oiv/dot_general | solution.py:50
  464.6 0.0 copy-done
  464.6 0.0 copy-done.2
  464.6 5.0 %bitcast_add_fusion = f32[6,128,512]{2,1,0:T(8,128)} fusion(f32[6,128,512,1]{2,1,3,0:T(8,128)S(1)} %fusion, f32[6,4,128,512]{3,2,1,0:T(8,128)S(1)} %bitcast.22, pred[6,4]{1,0:T(8,128)(4,1)S(1)} %compare_and_fusion.1, f32[6,4,128,128]{3,2,1,0:T(8,128)S(1)} %copy-done.2, f32[6,4]{1,0:T(8,128)S(1)} %convert_element_type.36), kind=kOutput, calls=%fused_computation.10 | convolution fusion | flops 2418278400 | bytes 11010168 | tf_op jit(solution)/shard_map/osij,osjv->oiv/dot_general | solution.py:50
  (11 shorter events, 0.1 us)
Async XLA Ops:
  7.4 2.8 copy-start.3
  7.4 4.8 %copy-start.1 = (f32[1,6,4,128,128]{4,3,2,1,0:T(8,128)S(1)}, f32[1,6,4,128,128]{4,3,2,1,0:T(8,128)}, u32[]{:S(2)}) copy-start(f32[1,6,4,128,128]{4,3,2,1,0:T(8,128)} %param.7) | copy-start | bytes 4718596
  7.4 142.2 %all-gather.7.cloned.1.call-start = ((), (), s32[]{:S(2)}) async-start(), calls=%async_computation.1 | async-start | bytes 4456448 | tf_op jit(solution)/shard_map/all_gather | solution.py:41
  9.4 276.0 %all-gather.5.cloned.1.call-start = ((), (), s32[]{:S(2)}) async-start(), calls=%async_computation | async-start | bytes 4456448 | tf_op jit(solution)/shard_map/all_gather | solution.py:41
  10.2 447.5 %all-reduce.3.cloned.1.call-start = ((), (), s32[]{:S(2)}) async-start(), calls=%async_computation.2 | async-start | bytes 6291456 | tf_op jit(solution)/shard_map/psum | solution.py:9
  14.2 0.7 copy-start.5
  14.2 0.7 copy-start.4
  457.6 7.0 %copy-start = (f32[24,128,512]{2,1,0:T(8,128)S(1)}, f32[24,128,512]{2,1,0:T(8,128)}, u32[]{:S(2)}) copy-start(f32[24,128,512]{2,1,0:T(8,128)} %gather_fusion) | copy-start | bytes 18874372
  457.6 7.0 %copy-start.2 = (f32[6,4,128,128]{3,2,1,0:T(8,128)S(1)}, f32[6,4,128,128]{3,2,1,0:T(8,128)}, u32[]{:S(2)}) copy-start(f32[6,4,128,128]{3,2,1,0:T(8,128)} %get-tuple-element.7) | copy-start | bytes 4718596
Sparse Core Ops, SparseCore 0:
  10.3 139.2 all-gather.6
  151.9 133.4 all-gather.4
Sparse Core Ops, SparseCore 1:
  14.4 443.2 all-reduce.2
where the time goes:
time: 477 us
  waiting for transfers between devices  430 us (90%)
  between operations  16.3 us (3%)
  local copies, waits for them, and re-layouts  15.1 us (3%)
  matrix products  12 us (3%)
    all_gather x2, waiting for transfers between devices, on_device(): lax.all_gather(integrals[which_section], 'row', axis=0, tiled=True)  263 us
    psum x1, waiting for transfers between devices, spread(): return lax.psum(kept, axis)  166 us
    dot_general x2, matrix products, on_device(): jnp.einsum('osij,osjv->oiv', amp_panel, picked, precision=lax.Precision.H...  12 us
    gather x2, local copies, waits for them, and re-layouts, on_device(): picked = jnp.take(row_tiles, tile_index, axis=0)  11.6 us
  transfers between devices with their start and end apart: 3, of which 3 were waited for; matrix products, arithmetic and copies ran while one was open for 3% of the time, Pallas kernels for 0%

commit v1 on v0

v1 whole, which is shorter than its diff:
```python
import functools

import jax
import jax.numpy as jnp
from jax import lax
from jax.experimental import pallas as pl
from jax.experimental.pallas import tpu as pltpu
from jax.sharding import PartitionSpec as P

MESH = pl.DeviceIdType.MESH
NX, NZ, NY, NH, NC = 4, 4, 8, 2, 2
TILE = 128
X_ROWS = 24
OFFSETS = (0, -1, 1, -2, 2, -3, 3)


class Copy:
    def __init__(self, src, dst, landing, send, recv, device, sends=None, receives=None):
        self.out = (src, dst, send, recv, device)
        self.into = (landing, landing, send, recv, device)
        self.sends, self.receives = sends, receives

    def start(self):
        guarded(self.sends, lambda: remote(*self.out).start())

    def wait_recv(self):
        guarded(self.receives, lambda: remote(*self.into).wait_recv())

    def wait_send(self):
        guarded(self.sends, lambda: remote(*self.out).wait_send())


def remote(src, dst, send, recv, device):
    return pltpu.make_async_remote_copy(
        src_ref=src, dst_ref=dst, send_sem=send, recv_sem=recv, device_id=device, device_id_type=MESH
    )


def guarded(condition, action):
    if condition is None:
        action()
    else:
        pl.when(condition)(action)


def multiply(occ_ref, pair_ref, first, panel, held, out_ref):
    sections, positions = pair_ref.shape
    slots = panel.shape[1] // (TILE * out_ref.shape[0] // TILE)
    bf, f32 = jnp.bfloat16, jnp.float32

    def split(value):
        high = value.astype(bf)
        return high, (value - high.astype(f32)).astype(bf)

    def one(o, carry):
        label = occ_ref[first + o]
        total = jnp.zeros((TILE, out_ref.shape[1]), f32)
        for k in range(sections):
            count = jnp.int32(0)
            index = [jnp.int32(0)] * slots
            for t in range(positions):
                match = pair_ref[k, t] == label
                for s in range(min(slots, t + 1)):
                    index[s] = jnp.where(match & (count == s), t, index[s])
                count = count + match.astype(jnp.int32)
            for pair in range(slots // 2):
                left, right = [], []
                for s in (2 * pair, 2 * pair + 1):
                    rows = pl.multiple_of((o * slots + s) * TILE, TILE)
                    tile = panel[k, pl.ds(rows, TILE), :]
                    left.append(jnp.where(count > s, tile, 0.0))
                    right.append(held[k, index[s] // NZ, index[s] % NZ])
                a_high, a_low = split(jnp.concatenate(left, axis=1))
                b_high, b_low = split(jnp.concatenate(right, axis=0))
                dot = functools.partial(jnp.dot, preferred_element_type=f32)
                total = total + (dot(a_high, b_high) + (dot(a_high, b_low) + dot(a_low, b_high)))
        out_ref[pl.ds(pl.multiple_of(o * TILE, TILE), TILE), :] = total
        return carry

    lax.fori_loop(0, out_ref.shape[0] // TILE, one, 0)


def kernel(owner_ref, occ_ref, pair_ref, amp_ref, int_ref, out_ref, held, panel, both, right_out, right_in,
           left_out, left_in, mine_out, other_in, local_sem, z_sem, x_sem, xf_sem, xz_sem, rs_sem, ag_sem, sib_sem,
           cross_sem):
    row, col = lax.axis_index("row"), lax.axis_index("col")
    x, z = row // NZ, row % NZ
    y, h, c = col // (NH * NC), (col // NC) % NH, col % NC

    def device(dx=0, dz=0, dy=0, flip_h=False, flip_c=False):
        h2 = 1 - h if flip_h else h
        c2 = 1 - c if flip_c else c
        return (((x + dx + NX) % NX) * NZ + z + dz, ((y + dy + NY) % NY) * (NH * NC) + h2 * NC + c2)

    sections = int_ref.shape[0]
    half = amp_ref.shape[0] // NC
    share = half // NY
    events = []

    def at(time, action):
        events.append((time, len(events), action))

    sent = []

    def go(copy):
        copy.start()
        sent.append(copy)

    barrier = pltpu.get_barrier_semaphore()
    partners = [device(dx=1), device(dx=-1), device(dy=1), device(dy=-1), device(flip_h=True), device(flip_c=True)]
    for partner in partners:
        pl.semaphore_signal(barrier, inc=1, device_id=partner, device_id_type=MESH)

    @pl.when(z > 0)
    def _():
        pl.semaphore_signal(barrier, inc=1, device_id=device(dz=-1), device_id_type=MESH)

    @pl.when(z < NZ - 1)
    def _():
        pl.semaphore_signal(barrier, inc=1, device_id=device(dz=1), device_id_type=MESH)

    own_ints = pltpu.make_async_copy(int_ref, held.at[:, x, z], local_sem.at[0])
    own_half = pltpu.make_async_copy(
        amp_ref.at[pl.ds(pl.multiple_of(c * half, 8), half), :], both.at[c], local_sem.at[1])
    own_ints.start()
    own_half.start()
    pl.semaphore_wait(barrier, len(partners) + (z > 0).astype(jnp.int32) + (z < NZ - 1).astype(jnp.int32))

    unit = 5.2 * (TILE - X_ROWS) / TILE

    zr = pl.ds(X_ROWS, TILE - X_ROWS)
    mid = (TILE - X_ROWS) // 16 * 8
    low, high = pl.ds(X_ROWS, mid), pl.ds(X_ROWS + mid, TILE - X_ROWS - mid)

    def z_copy(k, s, way):
        src = int_ref.at[k, zr] if s == 1 else held.at[k, x, z - way * (s - 1), zr]
        to = held.at[k, x, z - way * (s - 1), zr]
        frm = held.at[k, x, z - way * s, zr]
        if way > 0:
            sends, receives = (z < NZ - 1) & (z - (s - 1) >= 0), z - s >= 0
        else:
            sends, receives = (z > 0) & (z + (s - 1) <= NZ - 1), z + s <= NZ - 1
        w = 0 if way > 0 else 1
        return Copy(src, to, frm, z_sem.at[0, k, s - 1, w], z_sem.at[1, k, s - 1, w], device(dz=way), sends, receives)

    def x_copy(k, d, way):
        zz = z + d
        valid = None if d == 0 else (zz >= 0) & (zz <= NZ - 1)
        src = int_ref.at[k, zr] if d == 0 else held.at[k, x, zz, zr]
        w = 0 if way > 0 else 1
        return Copy(src, held.at[k, x, zz, zr], held.at[k, (x - way + NX) % NX, zz, zr],
                    x_sem.at[0, k, zz, w], x_sem.at[1, k, zz, w], device(dx=way), valid, valid)

    def x_forward(k, d, way):
        zz = z + d
        valid = None if d == 0 else (zz >= 0) & (zz <= NZ - 1)
        rows = low if way > 0 else high
        xs = (x - way + NX) % NX
        w = 2 if way > 0 else 3
        return Copy(held.at[k, xs, zz, rows], held.at[k, xs, zz, rows], held.at[k, (x + 2) % NX, zz, rows],
                    x_sem.at[0, k, zz, w], x_sem.at[1, k, zz, w], device(dx=way), valid, valid)

    def step_time(k, d):
        return 1.5 * unit * (2 * abs(d) + k)

    for k in range(sections):
        for way in (1, -1):
            at(0.01 + 0.1 * k, lambda k=k, way=way: go(z_copy(k, 1, way)))
            at(0.02 + 0.1 * k, lambda k=k, way=way: go(x_copy(k, 0, way)))
        for d in OFFSETS:
            if d:
                way, s = (1, -d) if d < 0 else (-1, d)

                def arrived(k=k, d=d, way=way, s=s):
                    z_copy(k, s, way).wait_recv()
                    if s < NZ - 1:
                        go(z_copy(k, s + 1, way))
                    for side in (1, -1):
                        go(x_copy(k, d, side))

                at((unit + 3.9 * X_ROWS / 24) * (s - 1) + unit * (k + 1), arrived)

            def passed(k=k, d=d):
                for side in (1, -1):
                    x_copy(k, d, side).wait_recv()
                    go(x_forward(k, d, side))

            def ended(k=k, d=d):
                for side in (1, -1):
                    x_forward(k, d, side).wait_recv()

            begin = max(step_time(k, d), (unit + 3.9 * X_ROWS / 24) * (abs(d) - 1) + unit * (k + 1) + 0.02 if d else 0.3)
            at(begin + unit, passed)
            at(begin + 1.8 * unit + 3, ended)

    if X_ROWS:
        xr = pl.ds(0, X_ROWS)
        cut = X_ROWS // 16 * 8
        xlow, xhigh = pl.ds(0, cut), pl.ds(cut, X_ROWS - cut)

        def f_copy(k, way):
            w = 0 if way > 0 else 1
            return Copy(int_ref.at[k, xr], held.at[k, x, z, xr], held.at[k, (x - way + NX) % NX, z, xr],
                        xf_sem.at[0, k, w], xf_sem.at[1, k, w], device(dx=way))

        def f_forward(k, way):
            rows = xlow if way > 0 else xhigh
            xs = (x - way + NX) % NX
            w = 2 if way > 0 else 3
            return Copy(held.at[k, xs, z, rows], held.at[k, xs, z, rows], held.at[k, (x + 2) % NX, z, rows],
                        xf_sem.at[0, k, w], xf_sem.at[1, k, w], device(dx=way))

        def fz_copy(k, s, way):
            to = held.at[k, :, z - way * (s - 1), xr]
            frm = held.at[k, :, z - way * s, xr]
            if way > 0:
                sends, receives = (z < NZ - 1) & (z - (s - 1) >= 0), z - s >= 0
            else:
                sends, receives = (z > 0) & (z + (s - 1) <= NZ - 1), z + s <= NZ - 1
            w = 0 if way > 0 else 1
            return Copy(to, to, frm, xz_sem.at[0, k, s - 1, w], xz_sem.at[1, k, s - 1, w], device(dz=way), sends, receives)

        for k in range(sections):
            for way in (1, -1):
                at(0.0 + 0.1 * k, lambda k=k, way=way: go(f_copy(k, way)))

            def near(k=k):
                for way in (1, -1):
                    f_copy(k, way).wait_recv()
                    go(f_forward(k, way))

            def far(k=k):
                for way in (1, -1):
                    f_forward(k, way).wait_recv()
                if k == 0:
                    own_ints.wait()
                for way in (1, -1):
                    go(fz_copy(k, 1, way))

            at(2.0 + k * 0.2, near)
            at(4.0 + k * 0.2, far)
            for s in range(1, NZ):

                def climb(k=k, s=s):
                    for way in (1, -1):
                        fz_copy(k, s, way).wait_recv()
                        if s < NZ - 1:
                            go(fz_copy(k, s + 1, way))

                at((2 * unit + 7.8 * X_ROWS / 24) * s + 2.0 * k, climb)
    else:
        at(4.0, own_ints.wait)

    def half_rows(core):
        return pl.ds(pl.multiple_of(core * half, 8), half)

    swap = Copy(amp_ref.at[half_rows(1 - c), :], both.at[c], both.at[1 - c], sib_sem.at[0, sections, 0],
                sib_sem.at[1, sections, 0], device(flip_c=True))

    owner_y = [owner_ref[k] // (NH * NC) for k in range(sections)]
    owner_h = [(owner_ref[k] // NC) % NH for k in range(sections)]
    owner_c = [owner_ref[k] % NC for k in range(sections)]

    def stored(k, j):
        rows = pl.ds(pl.multiple_of(j * share, 8), share)
        return jnp.where(owner_c[k] == 0, both[0, rows, :], both[1, rows, :])

    def rs_copy(k, i, way):
        w = 0 if way > 0 else 1
        src, dst = (right_out, right_in) if way > 0 else (left_out, left_in)
        return Copy(src.at[k, i], dst.at[k, i], dst.at[k, i], rs_sem.at[0, k, i, w], rs_sem.at[1, k, i, w], device(dy=way))

    def rs_send(k, i, way):
        j = (y + 4 - i) % NY if way > 0 else (y - 3 + i + NY) % NY
        src, dst = (right_out, right_in) if way > 0 else (left_out, left_in)
        value = stored(k, j)
        if i:
            value = jnp.where(owner_y[k] == y, value, dst[k, i - 1])
        src[k, i] = value
        go(rs_copy(k, i, way))

    def cross_copy(k):
        return Copy(mine_out.at[k], other_in.at[k], other_in.at[k], cross_sem.at[0, k], cross_sem.at[1, k],
                    device(flip_h=True))

    def share_rows(j, core):
        return pl.ds(pl.multiple_of(core * half + j * share, 8), share)

    def ag_copy(k, i, way):
        j = (y - way * i + NY) % NY
        g = (y - way * (i + 1) + NY) % NY
        w = 0 if way > 0 else 1
        return Copy(panel.at[k, share_rows(j, c), :], panel.at[k, share_rows(j, c), :], panel.at[k, share_rows(g, c), :],
                    ag_sem.at[0, k, i, w], ag_sem.at[1, k, i, w], device(dy=way))

    def sib_copy(k, d):
        j = (y - d + NY) % NY
        n = d + 3
        return Copy(panel.at[k, share_rows(j, c), :], panel.at[k, share_rows(j, c), :], panel.at[k, share_rows(j, 1 - c), :],
                    sib_sem.at[0, k, n], sib_sem.at[1, k, n], device(flip_c=True))

    def begin_rs():
        own_half.wait()
        swap.wait_recv()

    at(-0.5, lambda: go(swap))
    at(2.9, begin_rs)
    for k in range(sections):
        def first(k=k):
            for way in (1, -1):
                rs_send(k, 0, way)

        at(3.0 + 0.1 * k, first)
        for i in range(4):
            def advance(k=k, i=i):
                for way in (1, -1):
                    if way > 0 or i < 3:
                        rs_copy(k, i, way).wait_recv()
                    if i < (3 if way > 0 else 2):
                        rs_send(k, i + 1, way)
                if i == 3:
                    ahead = (owner_y[k] - y + NY) % NY
                    value = jnp.where(ahead == 0, stored(k, y), jnp.where(ahead <= 3, left_in[k, 2], right_in[k, 3]))
                    mine_out[k] = value
                    go(cross_copy(k))

            at(4.0 + 4.5 * (i + 1) + 2.0 * k, advance)

        def crossed(k=k):
            cross_copy(k).wait_recv()
            panel[k, share_rows(y, c), :] = jnp.where(owner_h[k] == h, mine_out[k], other_in[k])
            for way in (1, -1):
                go(ag_copy(k, 0, way))
            go(sib_copy(k, 0))

        at(28.0 + 2.0 * k, crossed)
        for i in range(4):
            def gathered(k=k, i=i):
                for way in (1, -1):
                    if way < 0 and i == 3:
                        continue
                    ag_copy(k, i, way).wait_recv()
                    if i < (3 if way > 0 else 2):
                        go(ag_copy(k, i + 1, way))
                    go(sib_copy(k, way * (i + 1)))

            at(28.0 + 4.5 * (i + 1) + 2.0 * k, gathered)

        def complete(k=k):
            for d in range(-3, 5):
                sib_copy(k, d).wait_recv()

        at(50.0 + k, complete)

    for _, _, action in sorted(events, key=lambda event: event[:2]):
        action()
    multiply(occ_ref, pair_ref, row * (out_ref.shape[0] // TILE), panel, held, out_ref)
    for copy in sent:
        copy.wait_send()


def on_device(amplitudes, integrals, owner_column, occ_irrep, pair_irrep):
    tiles_here, slots, tile = amplitudes.shape[1:4]
    sections, _, columns = integrals.shape
    rows = tiles_here * slots * tile
    half, share = rows // NC, rows // NC // NY
    f32 = jnp.float32
    dma = pltpu.SemaphoreType.DMA
    smem = pl.BlockSpec(memory_space=pltpu.SMEM)
    return pl.pallas_call(
        kernel,
        out_shape=jax.ShapeDtypeStruct((tiles_here * tile, columns), f32),
        in_specs=[smem, smem, smem, pl.BlockSpec(memory_space=pl.ANY), pl.BlockSpec(memory_space=pl.ANY)],
        out_specs=pl.BlockSpec(memory_space=pltpu.VMEM),
        scratch_shapes=[
            pltpu.VMEM((sections, NX, NZ, tile, columns), f32),
            pltpu.VMEM((sections, rows, tile), f32),
            pltpu.VMEM((NC, half, tile), f32),
            pltpu.VMEM((sections, 4, share, tile), f32),
            pltpu.VMEM((sections, 4, share, tile), f32),
            pltpu.VMEM((sections, 3, share, tile), f32),
            pltpu.VMEM((sections, 3, share, tile), f32),
            pltpu.VMEM((sections, share, tile), f32),
            pltpu.VMEM((sections, share, tile), f32),
            dma((2,)),
            dma((2, sections, 3, 2)),
            dma((2, sections, 4, 4)),
            dma((2, sections, 4)),
            dma((2, sections, 3, 2)),
            dma((2, sections, 4, 2)),
            dma((2, sections, 4, 2)),
            dma((2, sections + 1, 8)),
            dma((2, sections)),
        ],
        compiler_params=pltpu.CompilerParams(
            collective_id=0, has_side_effects=True, vmem_limit_bytes=48 * 1024 * 1024
        ),
        name="ladder",
    )(owner_column, occ_irrep, pair_irrep, amplitudes.reshape(rows, tile), integrals)


def solution(mesh):
    return jax.shard_map(
        on_device,
        mesh=mesh,
        in_specs=(P("col", "row", None, None, None), P(None, "row", "col"), P(), P(), P()),
        out_specs=P("row", "col"),
        check_vma=False,
    )
```

time: 477 us -> 104 us (0.22)
  the two profiles are of different devices: /device:TPU:1 before, /device:TPU:65 now
where the time goes in v1:
time: 104 us; the launch traced here: 103 us
  Pallas kernels  97.7 us (94%)
  local copies, waits for them, and re-layouts  5.58 us (5%)
    pallas_call x1, Pallas kernels, on_device(): pl.pallas_call(kernel, out_shape=jax.ShapeDtypeStruct((tiles_here * tile,...  97.7 us
    unnamed x11, local copies, waits for them, and re-layouts  5.58 us

profile of v1, /device:TPU:65, one launch (start us, length us, event | category | flops | bytes accessed | tf_op | source)
XLA Modules:
  0.0 103.3 jit_solution(16238164935332403571)
XLA Ops:
  0.0 0.0 copy-start
  0.0 1.4 %copy-done = f32[1,6,4,128,128]{4,3,2,1,0:T(8,128)S(1)} copy-done((f32[1,6,4,128,128]{4,3,2,1,0:T(8,128)S(1)}, f32[1,6,4,128,128]{4,3,2,1,0:T(8,128)}, u32[]{:S(2)}) %copy-start) | copy-done | bytes 1572888
  1.4 0.0 copy-start.1
  1.4 1.0 %copy-done.1 = f32[2,128,512]{2,1,0:T(8,128)S(1)} copy-done((f32[2,128,512]{2,1,0:T(8,128)S(1)}, f32[2,128,512]{2,1,0:T(8,128)}, u32[]{:S(2)}) %copy-start.1) | copy-done | bytes 524312
  2.5 0.0 copy-start.2
  2.5 0.7 copy-done.2
  3.1 0.0 copy-start.3
  3.1 0.7 copy-done.3
  3.8 0.0 copy-start.4
  3.8 0.7 copy-done.4
  4.4 97.7 %ladder.1 = f32[768,512]{1,0:T(8,128)S(1)} custom-call(s32[2]{0:T(128)S(1)} %copy-done.3, s32[96]{0:T(128)S(1)} %copy-done.4, s32[2,16]{1,0:T(2,128)S(1)} %copy-done.2, f32[3072,128]{1,0:T(8,128)S(1)} %bitcast.1, f32[2,128,512]{2,1,0:T(8,128)S(1)} %copy-done.1), custom_call_target="tpu_custom_call" | custom-call | tf_op jit(solution)/shard_map/ladder/pallas_call | solution.py:370
  102.1 1.1 %copy.7 = f32[768,512]{1,0:T(8,128)} copy(f32[768,512]{1,0:T(8,128)S(1)} %ladder.1) | data formatting | bytes 3145728
Async XLA Ops:
  0.0 1.4 %copy-start = (f32[1,6,4,128,128]{4,3,2,1,0:T(8,128)S(1)}, f32[1,6,4,128,128]{4,3,2,1,0:T(8,128)}, u32[]{:S(2)}) copy-start(f32[1,6,4,128,128]{4,3,2,1,0:T(8,128)} %param.5) | copy-start | bytes 4718596
  1.4 1.0 %copy-start.1 = (f32[2,128,512]{2,1,0:T(8,128)S(1)}, f32[2,128,512]{2,1,0:T(8,128)}, u32[]{:S(2)}) copy-start(f32[2,128,512]{2,1,0:T(8,128)} %int_ref.1) | copy-start | bytes 1572868
  2.5 0.7 copy-start.2
  3.1 0.7 copy-start.3
  3.8 0.7 copy-start.4

commit v2 on v1

--- a/solution.py
+++ b/solution.py
@@ -12,6 +12,22 @@
 TILE = 128
 X_ROWS = 24
 OFFSETS = (0, -1, 1, -2, 2, -3, 3)
+ORDER = (
+    ('swap',), ('z', 0, 1, -1), ('rs', 0, 0, 1), ('z', 0, 1, 1), ('rs', 0, 0, -1), ('z', 1, 1, -1),
+    ('rs', 0, 1, -1), ('rs', 1, 0, 1), ('rs', 1, 0, -1), ('f', 0, 1), ('x', 0, 0, -1), ('f', 0, -1), ('z', 1, 1, 1),
+    ('rs', 0, 1, 1), ('z', 0, 2, 1), ('f', 1, 1), ('rs', 1, 1, 1), ('z', 0, 2, -1), ('rs', 0, 2, 1),
+    ('rs', 1, 2, 1), ('rs', 1, 1, -1), ('rs', 0, 2, -1), ('f', 1, -1), ('rs', 0, 3, 1), ('z', 0, 3, -1),
+    ('rs', 1, 2, -1), ('x', 0, 0, 1), ('x', 1, 0, 1), ('rs', 1, 3, 1), ('x', 0, -1, -1), ('x', 0, 3, 1), ('fz', 0),
+    ('x', 1, 1, 1), ('cross', 0), ('z', 1, 2, -1), ('ag', 0, 0, 1), ('x', 1, 0, -1), ('z', 1, 2, 1), ('x', 0, 2, 1),
+    ('x', 0, -2, -1), ('x', 0, 2, -1), ('fz', 1), ('cross', 1), ('ag', 0, 1, 1), ('x', 0, -1, 1), ('z', 1, 3, 1),
+    ('x', 0, 1, -1), ('ag', 1, 0, -1), ('ag', 0, 0, -1), ('x', 0, 1, 1), ('c', 0, 1, -1), ('ag', 1, 0, 1),
+    ('z', 0, 3, 1), ('c', 0, 1, 1), ('c', 1, 1, -1), ('x', 1, -2, -1), ('ag', 1, 1, 1), ('x', 1, -2, 1),
+    ('ag', 0, 2, 1), ('c', 1, 1, 1), ('x', 1, 2, 1), ('ag', 0, 1, -1), ('ag', 1, 1, -1), ('x', 0, -2, 1),
+    ('x', 1, -3, -1), ('x', 1, 2, -1), ('x', 1, -1, -1), ('z', 1, 3, -1), ('ag', 0, 2, -1), ('x', 1, -1, 1),
+    ('ag', 1, 2, 1), ('x', 0, 3, -1), ('x', 1, 3, 1), ('x', 1, 1, -1), ('ag', 0, 3, 1), ('c', 1, 2, -1),
+    ('c', 0, 2, 1), ('ag', 1, 3, 1), ('x', 1, -3, 1), ('c', 0, 2, -1), ('ag', 1, 2, -1), ('x', 0, -3, 1),
+    ('x', 1, 3, -1), ('x', 0, -3, -1), ('c', 1, 2, 1),
+)
 
 
 class Copy:
@@ -95,12 +111,7 @@
     sections = int_ref.shape[0]
     half = amp_ref.shape[0] // NC
     share = half // NY
-    events = []
-
-    def at(time, action):
-        events.append((time, len(events), action))
-
-    sent = []
+    events, last, sent = {}, [], []
 
     def go(copy):
         copy.start()
@@ -125,8 +136,6 @@
     own_ints.start()
     own_half.start()
     pl.semaphore_wait(barrier, len(partners) + (z > 0).astype(jnp.int32) + (z < NZ - 1).astype(jnp.int32))
-
-    unit = 5.2 * (TILE - X_ROWS) / TILE
 
     zr = pl.ds(X_ROWS, TILE - X_ROWS)
     mid = (TILE - X_ROWS) // 16 * 8
@@ -160,13 +169,7 @@
         return Copy(held.at[k, xs, zz, rows], held.at[k, xs, zz, rows], held.at[k, (x + 2) % NX, zz, rows],
                     x_sem.at[0, k, zz, w], x_sem.at[1, k, zz, w], device(dx=way), valid, valid)
 
-    def step_time(k, d):
-        return 1.5 * unit * (2 * abs(d) + k)
-
     for k in range(sections):
-        for way in (1, -1):
-            at(0.01 + 0.1 * k, lambda k=k, way=way: go(z_copy(k, 1, way)))
-            at(0.02 + 0.1 * k, lambda k=k, way=way: go(x_copy(k, 0, way)))
         for d in OFFSETS:
             if d:
                 way, s = (1, -d) if d < 0 else (-1, d)
@@ -178,20 +181,15 @@
                     for side in (1, -1):
                         go(x_copy(k, d, side))
 
-                at((unit + 3.9 * X_ROWS / 24) * (s - 1) + unit * (k + 1), arrived)
-
-            def passed(k=k, d=d):
-                for side in (1, -1):
-                    x_copy(k, d, side).wait_recv()
-                    go(x_forward(k, d, side))
-
-            def ended(k=k, d=d):
-                for side in (1, -1):
-                    x_forward(k, d, side).wait_recv()
-
-            begin = max(step_time(k, d), (unit + 3.9 * X_ROWS / 24) * (abs(d) - 1) + unit * (k + 1) + 0.02 if d else 0.3)
-            at(begin + unit, passed)
-            at(begin + 1.8 * unit + 3, ended)
+                events["z", k, s, way] = arrived
+            for way in (1, -1):
+
+                def passed(k=k, d=d, way=way):
+                    x_copy(k, d, way).wait_recv()
+                    go(x_forward(k, d, way))
+
+                events["x", k, d, way] = passed
+                last.append(x_forward(k, d, way))
 
     if X_ROWS:
         xr = pl.ds(0, X_ROWS)
@@ -222,34 +220,28 @@
 
         for k in range(sections):
             for way in (1, -1):
-                at(0.0 + 0.1 * k, lambda k=k, way=way: go(f_copy(k, way)))
-
-            def near(k=k):
-                for way in (1, -1):
+
+                def near(k=k, way=way):
                     f_copy(k, way).wait_recv()
                     go(f_forward(k, way))
+
+                events["f", k, way] = near
+                for s in range(1, NZ - 1):
+
+                    def climb(k=k, s=s, way=way):
+                        fz_copy(k, s, way).wait_recv()
+                        go(fz_copy(k, s + 1, way))
+
+                    events["c", k, s, way] = climb
+                last.append(fz_copy(k, NZ - 1, way))
 
             def far(k=k):
                 for way in (1, -1):
                     f_forward(k, way).wait_recv()
-                if k == 0:
-                    own_ints.wait()
                 for way in (1, -1):
                     go(fz_copy(k, 1, way))
 
-            at(2.0 + k * 0.2, near)
-            at(4.0 + k * 0.2, far)
-            for s in range(1, NZ):
-
-                def climb(k=k, s=s):
-                    for way in (1, -1):
-                        fz_copy(k, s, way).wait_recv()
-                        if s < NZ - 1:
-                            go(fz_copy(k, s + 1, way))
-
-                at((2 * unit + 7.8 * X_ROWS / 24) * s + 2.0 * k, climb)
-    else:
-        at(4.0, own_ints.wait)
+            events["fz", k] = far
 
     def half_rows(core):
         return pl.ds(pl.multiple_of(core * half, 8), half)
@@ -299,32 +291,41 @@
         return Copy(panel.at[k, share_rows(j, c), :], panel.at[k, share_rows(j, c), :], panel.at[k, share_rows(j, 1 - c), :],
                     sib_sem.at[0, k, n], sib_sem.at[1, k, n], device(flip_c=True))
 
-    def begin_rs():
+    def swapped():
         own_half.wait()
         swap.wait_recv()
-
-    at(-0.5, lambda: go(swap))
-    at(2.9, begin_rs)
-    for k in range(sections):
-        def first(k=k):
+        for k in range(sections):
             for way in (1, -1):
                 rs_send(k, 0, way)
 
-        at(3.0 + 0.1 * k, first)
-        for i in range(4):
-            def advance(k=k, i=i):
-                for way in (1, -1):
-                    if way > 0 or i < 3:
-                        rs_copy(k, i, way).wait_recv()
-                    if i < (3 if way > 0 else 2):
+    events["swap",] = swapped
+    steps = {1: NY // 2, -1: NY // 2 - 1}
+    for k in range(sections):
+        ended = []
+        for way in (1, -1):
+            for i in range(steps[way]):
+
+                def advance(k=k, i=i, way=way, ended=ended):
+                    rs_copy(k, i, way).wait_recv()
+                    if i < steps[way] - 1:
                         rs_send(k, i + 1, way)
-                if i == 3:
-                    ahead = (owner_y[k] - y + NY) % NY
-                    value = jnp.where(ahead == 0, stored(k, y), jnp.where(ahead <= 3, left_in[k, 2], right_in[k, 3]))
-                    mine_out[k] = value
-                    go(cross_copy(k))
-
-            at(4.0 + 4.5 * (i + 1) + 2.0 * k, advance)
+                    else:
+                        ended.append(way)
+                    if len(ended) == 2:
+                        ended.append(0)
+                        ahead = (owner_y[k] - y + NY) % NY
+                        mine_out[k] = jnp.where(
+                            ahead == 0, stored(k, y), jnp.where(ahead <= 3, left_in[k, 2], right_in[k, 3]))
+                        go(cross_copy(k))
+
+                def gathered(k=k, i=i, way=way):
+                    ag_copy(k, i, way).wait_recv()
+                    if i < steps[way] - 1:
+                        go(ag_copy(k, i + 1, way))
+                    go(sib_copy(k, way * (i + 1)))
+
+                events["rs", k, i, way] = advance
+                events["ag", k, i, way] = gathered
 
         def crossed(k=k):
             cross_copy(k).wait_recv()
@@ -333,27 +334,27 @@
                 go(ag_copy(k, 0, way))
             go(sib_copy(k, 0))
 
-        at(28.0 + 2.0 * k, crossed)
-        for i in range(4):
-            def gathered(k=k, i=i):
-                for way in (1, -1):
-                    if way < 0 and i == 3:
-                        continue
-                    ag_copy(k, i, way).wait_recv()
-                    if i < (3 if way > 0 else 2):
-                        go(ag_copy(k, i + 1, way))
-                    go(sib_copy(k, way * (i + 1)))
-
-            at(28.0 + 4.5 * (i + 1) + 2.0 * k, gathered)
-
-        def complete(k=k):
-            for d in range(-3, 5):
-                sib_copy(k, d).wait_recv()
-
-        at(50.0 + k, complete)
-
-    for _, _, action in sorted(events, key=lambda event: event[:2]):
-        action()
+        events["cross", k] = crossed
+        last.extend(sib_copy(k, d) for d in range(-3, 5))
+
+    go(swap)
+    for k in range(sections):
+        for way in (1, -1):
+            go(z_copy(k, 1, way))
+        for way in (1, -1):
+            go(x_copy(k, 0, way))
+    if X_ROWS:
+        for k in range(sections):
+            for way in (1, -1):
+                go(f_copy(k, way))
+        own_ints.wait()
+    for key in ORDER:
+        events.pop(key)()
+    if not X_ROWS:
+        own_ints.wait()
+    assert not events
+    for copy in last:
+        copy.wait_recv()
     multiply(occ_ref, pair_ref, row * (out_ref.shape[0] // TILE), panel, held, out_ref)
     for copy in sent:
         copy.wait_send()
@@ -393,7 +394,7 @@
             dma((2, sections)),
         ],
         compiler_params=pltpu.CompilerParams(
-            collective_id=0, has_side_effects=True, vmem_limit_bytes=48 * 1024 * 1024
+            collective_id=0, has_side_effects=True, vmem_limit_bytes=60 * 1024 * 1024
         ),
         name="ladder",
     )(owner_column, occ_irrep, pair_irrep, amplitudes.reshape(rows, tile), integrals)

time: 104 us -> 88.3 us (0.85)
  the two profiles are of different devices: /device:TPU:65 before, /device:TPU:1 now
where the time goes in v2:
time: 88.3 us; the launch traced here: 87.2 us
  Pallas kernels  84.5 us (96%)
  local copies, waits for them, and re-layouts  2.67 us (3%)
    pallas_call x1, Pallas kernels, on_device(): pl.pallas_call(kernel, out_shape=jax.ShapeDtypeStruct((tiles_here * tile,...  84.5 us
    unnamed x1, local copies, waits for them, and re-layouts  2.67 us

profile of v2, /device:TPU:1, one launch (start us, length us, event | category | flops | bytes accessed | tf_op | source)
XLA Modules:
  0.0 87.2 jit_solution(4145833680258817610)
XLA Ops:
  0.0 84.5 %ladder.1 = f32[768,512]{1,0:T(8,128)} custom-call(s32[2]{0:T(128)} %owner_ref.1, s32[96]{0:T(128)} %occ_ref.1, s32[2,16]{1,0:T(2,128)} %pair_ref.1, f32[3072,128]{1,0:T(8,128)} %bitcast.1, f32[2,128,512]{2,1,0:T(8,128)} %int_ref.1), custom_call_target="tpu_custom_call" | custom-call | tf_op jit(solution)/shard_map/ladder/pallas_call | solution.py:371
  84.5 2.7 %copy.7 = f32[768,512]{1,0:T(8,128)} copy(f32[768,512]{1,0:T(8,128)} %ladder.1) | data formatting | bytes 3145728

commit v3 on v2

v3 whole, which is shorter than its diff:
```python
import functools

import jax
import jax.numpy as jnp
from jax import lax
from jax.experimental import pallas as pl
from jax.experimental.pallas import tpu as pltpu
from jax.sharding import PartitionSpec as P

MESH = pl.DeviceIdType.MESH
NX, NZ, NY, NH, NC = 4, 4, 8, 2, 2
TILE = 128
X_ROWS = (24, 16)
OFFSETS = (0, -1, 1, -2, 2, -3, 3)
ORDER = (
    ('fs', 1), ('swap',), ('z', 0, 1, -1), ('fs', 0), ('rs', 0, 0, 1), ('z', 0, 1, 1), ('z', 1, 1, 1),
    ('rs', 1, 0, 1), ('z', 1, 1, -1), ('rs', 0, 0, -1), ('rs', 1, 0, -1), ('rs', 0, 1, 1), ('rs', 1, 1, 1),
    ('z', 0, 2, 1), ('f', 0, -1), ('rs', 0, 1, -1), ('rs', 0, 2, 1), ('z', 0, 2, -1), ('rs', 1, 2, 1), ('f', 0, 1),
    ('f', 1, -1), ('f', 1, 1), ('rs', 1, 1, -1), ('x', 1, 0, 1), ('x', 1, 0, -1), ('rs', 0, 2, -1), ('rs', 0, 3, 1),
    ('z', 0, 3, 1), ('rs', 1, 3, 1), ('x', 0, 0, 1), ('rs', 1, 2, -1), ('z', 1, 2, 1), ('z', 0, 3, -1),
    ('z', 1, 2, -1), ('x', 0, 3, -1), ('x', 0, -1, -1), ('x', 0, 1, 1), ('cross', 0), ('fz', 0), ('x', 0, -3, -1),
    ('x', 0, -3, 1), ('x', 0, 1, -1), ('cross', 1), ('x', 1, 1, 1), ('x', 0, -2, 1), ('z', 1, 3, -1),
    ('z', 1, 3, 1), ('ag', 0, 0, 1), ('x', 0, 0, -1), ('x', 0, -1, 1), ('x', 0, 2, -1), ('x', 1, -1, 1),
    ('x', 1, 1, -1), ('fz', 1), ('ag', 1, 0, -1), ('c', 0, 1, -1), ('ag', 1, 0, 1), ('x', 0, -2, -1),
    ('c', 0, 1, 1), ('x', 1, -1, -1), ('ag', 0, 0, -1), ('ag', 0, 1, 1), ('x', 1, 2, -1), ('c', 1, 1, -1),
    ('x', 0, 2, 1), ('ag', 1, 1, 1), ('ag', 1, 1, -1), ('x', 1, -2, -1), ('c', 1, 1, 1), ('ag', 0, 2, 1),
    ('x', 0, 3, 1), ('ag', 0, 1, -1), ('x', 1, 2, 1), ('c', 0, 2, 1), ('c', 0, 2, -1), ('x', 1, -3, 1),
    ('ag', 1, 2, 1), ('ag', 0, 2, -1), ('c', 1, 2, 1), ('x', 1, -3, -1), ('c', 1, 2, -1), ('x', 1, -2, 1),
    ('ag', 1, 2, -1), ('x', 1, 3, -1), ('x', 1, 3, 1), ('ag', 0, 3, 1), ('ag', 1, 3, 1),
)


class Copy:
    def __init__(self, src, dst, landing, send, recv, device, sends=None, receives=None):
        self.out = (src, dst, send, recv, device)
        self.into = (landing, landing, send, recv, device)
        self.sends, self.receives = sends, receives

    def start(self):
        guarded(self.sends, lambda: remote(*self.out).start())

    def wait_recv(self):
        guarded(self.receives, lambda: remote(*self.into).wait_recv())

    def wait_send(self):
        guarded(self.sends, lambda: remote(*self.out).wait_send())


def remote(src, dst, send, recv, device):
    return pltpu.make_async_remote_copy(
        src_ref=src, dst_ref=dst, send_sem=send, recv_sem=recv, device_id=device, device_id_type=MESH
    )


def guarded(condition, action):
    if condition is None:
        action()
    else:
        pl.when(condition)(action)


def multiply(k, occ_ref, pair_ref, first, panel, held, out_ref):
    positions = pair_ref.shape[1]
    slots = panel.shape[1] // out_ref.shape[0]
    bf, f32 = jnp.bfloat16, jnp.float32

    def split(value):
        high = value.astype(bf)
        return high, (value - high.astype(f32)).astype(bf)

    def one(o, carry):
        label = occ_ref[first + o]
        here = pl.ds(pl.multiple_of(o * TILE, TILE), TILE)
        count = jnp.int32(0)
        index = [jnp.int32(0)] * slots
        for t in range(positions):
            match = pair_ref[k, t] == label
            for s in range(min(slots, t + 1)):
                index[s] = jnp.where(match & (count == s), t, index[s])
            count = count + match.astype(jnp.int32)
        total = None if k == 0 else out_ref[here, :]
        for pair in range(slots // 2):
            left, right = [], []
            for s in (2 * pair, 2 * pair + 1):
                rows = pl.multiple_of((o * slots + s) * TILE, TILE)
                tile = panel[k, pl.ds(rows, TILE), :]
                left.append(jnp.where(count > s, tile, 0.0))
                right.append(held[index[s] // NZ, index[s] % NZ])
            a_high, a_low = split(jnp.concatenate(left, axis=1))
            b_high, b_low = split(jnp.concatenate(right, axis=0))
            dot = functools.partial(jnp.dot, preferred_element_type=f32)
            part = dot(a_high, b_high) + (dot(a_high, b_low) + dot(a_low, b_high))
            total = part if total is None else total + part
        out_ref[here, :] = total
        return carry

    lax.fori_loop(0, out_ref.shape[0] // TILE, one, 0)


def kernel(owner_ref, occ_ref, pair_ref, amp_ref, int_ref, out_ref, held_0, held_1, panel, both, right_out, right_in,
           left_out, left_in, mine_out, other_in, local_sem, z_sem, x_sem, xf_sem, xz_sem, rs_sem, ag_sem, sib_sem,
           cross_sem):
    row, col = lax.axis_index("row"), lax.axis_index("col")
    x, z = row // NZ, row % NZ
    y, h, c = col // (NH * NC), (col // NC) % NH, col % NC

    def device(dx=0, dz=0, dy=0, flip_h=False, flip_c=False):
        h2 = 1 - h if flip_h else h
        c2 = 1 - c if flip_c else c
        return (((x + dx + NX) % NX) * NZ + z + dz, ((y + dy + NY) % NY) * (NH * NC) + h2 * NC + c2)

    held = (held_0, held_1)
    sections = int_ref.shape[0]
    half = amp_ref.shape[0] // NC
    share = half // NY
    events, last, sent = {}, [[] for _ in range(sections)], []

    def go(copy):
        copy.start()
        sent.append(copy)

    barrier = pltpu.get_barrier_semaphore()
    partners = [device(dx=1), device(dx=-1), device(dy=1), device(dy=-1), device(flip_h=True), device(flip_c=True)]
    for partner in partners:
        pl.semaphore_signal(barrier, inc=1, device_id=partner, device_id_type=MESH)

    @pl.when(z > 0)
    def _():
        pl.semaphore_signal(barrier, inc=1, device_id=device(dz=-1), device_id_type=MESH)

    @pl.when(z < NZ - 1)
    def _():
        pl.semaphore_signal(barrier, inc=1, device_id=device(dz=1), device_id_type=MESH)

    own_ints = [pltpu.make_async_copy(int_ref.at[k], held[k].at[x, z], local_sem.at[1 + k]) for k in range(sections)]
    own_half = pltpu.make_async_copy(
        amp_ref.at[pl.ds(pl.multiple_of(c * half, 8), half), :], both.at[c], local_sem.at[0])
    for copy in own_ints:
        copy.start()
    own_half.start()
    pl.semaphore_wait(barrier, len(partners) + (z > 0).astype(jnp.int32) + (z < NZ - 1).astype(jnp.int32))

    mid = [(TILE - first) // 16 * 8 for first in X_ROWS]
    zr = [pl.ds(first, TILE - first) for first in X_ROWS]
    low = [pl.ds(first, m) for first, m in zip(X_ROWS, mid)]
    high = [pl.ds(first + m, TILE - first - m) for first, m in zip(X_ROWS, mid)]

    def z_copy(k, s, way):
        src = int_ref.at[k, zr[k]] if s == 1 else held[k].at[x, z - way * (s - 1), zr[k]]
        to = held[k].at[x, z - way * (s - 1), zr[k]]
        frm = held[k].at[x, z - way * s, zr[k]]
        if way > 0:
            sends, receives = (z < NZ - 1) & (z - (s - 1) >= 0), z - s >= 0
        else:
            sends, receives = (z > 0) & (z + (s - 1) <= NZ - 1), z + s <= NZ - 1
        w = 0 if way > 0 else 1
        return Copy(src, to, frm, z_sem.at[0, k, s - 1, w], z_sem.at[1, k, s - 1, w], device(dz=way), sends, receives)

    def x_copy(k, d, way):
        zz = z + d
        valid = None if d == 0 else (zz >= 0) & (zz <= NZ - 1)
        src = int_ref.at[k, zr[k]] if d == 0 else held[k].at[x, zz, zr[k]]
        w = 0 if way > 0 else 1
        return Copy(src, held[k].at[x, zz, zr[k]], held[k].at[(x - way + NX) % NX, zz, zr[k]],
                    x_sem.at[0, k, zz, w], x_sem.at[1, k, zz, w], device(dx=way), valid, valid)

    def x_forward(k, d, way):
        zz = z + d
        valid = None if d == 0 else (zz >= 0) & (zz <= NZ - 1)
        rows = low[k] if way > 0 else high[k]
        xs = (x - way + NX) % NX
        w = 2 if way > 0 else 3
        return Copy(held[k].at[xs, zz, rows], held[k].at[xs, zz, rows], held[k].at[(x + 2) % NX, zz, rows],
                    x_sem.at[0, k, zz, w], x_sem.at[1, k, zz, w], device(dx=way), valid, valid)

    for k in range(sections):
        for d in OFFSETS:
            if d:
                way, s = (1, -d) if d < 0 else (-1, d)

                def arrived(k=k, d=d, way=way, s=s):
                    z_copy(k, s, way).wait_recv()
                    if s < NZ - 1:
                        go(z_copy(k, s + 1, way))
                    for side in (1, -1):
                        go(x_copy(k, d, side))

                events["z", k, s, way] = arrived
            for way in (1, -1):

                def passed(k=k, d=d, way=way):
                    x_copy(k, d, way).wait_recv()
                    go(x_forward(k, d, way))

                events["x", k, d, way] = passed
                last[k].append(x_forward(k, d, way))

    cut = [first // 16 * 8 for first in X_ROWS]
    xr = [pl.ds(0, first) for first in X_ROWS]
    xlow = [pl.ds(0, m) for m in cut]
    xhigh = [pl.ds(m, first - m) for first, m in zip(X_ROWS, cut)]

    def f_copy(k, way):
        w = 0 if way > 0 else 1
        return Copy(int_ref.at[k, xr[k]], held[k].at[x, z, xr[k]], held[k].at[(x - way + NX) % NX, z, xr[k]],
                    xf_sem.at[0, k, w], xf_sem.at[1, k, w], device(dx=way))

    def f_forward(k, way):
        rows = xlow[k] if way > 0 else xhigh[k]
        xs = (x - way + NX) % NX
        w = 2 if way > 0 else 3
        return Copy(held[k].at[xs, z, rows], held[k].at[xs, z, rows], held[k].at[(x + 2) % NX, z, rows],
                    xf_sem.at[0, k, w], xf_sem.at[1, k, w], device(dx=way))

    def fz_copy(k, s, way):
        to = held[k].at[:, z - way * (s - 1), xr[k]]
        frm = held[k].at[:, z - way * s, xr[k]]
        if way > 0:
            sends, receives = (z < NZ - 1) & (z - (s - 1) >= 0), z - s >= 0
        else:
            sends, receives = (z > 0) & (z + (s - 1) <= NZ - 1), z + s <= NZ - 1
        w = 0 if way > 0 else 1
        return Copy(to, to, frm, xz_sem.at[0, k, s - 1, w], xz_sem.at[1, k, s - 1, w], device(dz=way), sends, receives)

    for k in range(sections):

        def spread(k=k):
            for way in (1, -1):
                go(f_copy(k, way))

        events["fs", k] = spread
        for way in (1, -1):

            def near(k=k, way=way):
                f_copy(k, way).wait_recv()
                go(f_forward(k, way))

            events["f", k, way] = near
            for s in range(1, NZ - 1):

                def climb(k=k, s=s, way=way):
                    fz_copy(k, s, way).wait_recv()
                    go(fz_copy(k, s + 1, way))

                events["c", k, s, way] = climb
            last[k].append(fz_copy(k, NZ - 1, way))

        def far(k=k):
            own_ints[k].wait()
            for way in (1, -1):
                f_forward(k, way).wait_recv()
            for way in (1, -1):
                go(fz_copy(k, 1, way))

        events["fz", k] = far

    def half_rows(core):
        return pl.ds(pl.multiple_of(core * half, 8), half)

    swap = Copy(amp_ref.at[half_rows(1 - c), :], both.at[c], both.at[1 - c], sib_sem.at[0, sections, 0],
                sib_sem.at[1, sections, 0], device(flip_c=True))

    owner_y = [owner_ref[k] // (NH * NC) for k in range(sections)]
    owner_h = [(owner_ref[k] // NC) % NH for k in range(sections)]
    owner_c = [owner_ref[k] % NC for k in range(sections)]

    def stored(k, j):
        rows = pl.ds(pl.multiple_of(j * share, 8), share)
        return jnp.where(owner_c[k] == 0, both[0, rows, :], both[1, rows, :])

    def rs_copy(k, i, way):
        w = 0 if way > 0 else 1
        src, dst = (right_out, right_in) if way > 0 else (left_out, left_in)
        return Copy(src.at[k, i], dst.at[k, i], dst.at[k, i], rs_sem.at[0, k, i, w], rs_sem.at[1, k, i, w], device(dy=way))

    def rs_send(k, i, way):
        j = (y + 4 - i) % NY if way > 0 else (y - 3 + i + NY) % NY
        src, dst = (right_out, right_in) if way > 0 else (left_out, left_in)
        value = stored(k, j)
        if i:
            value = jnp.where(owner_y[k] == y, value, dst[k, i - 1])
        src[k, i] = value
        go(rs_copy(k, i, way))

    def cross_copy(k):
        return Copy(mine_out.at[k], other_in.at[k], other_in.at[k], cross_sem.at[0, k], cross_sem.at[1, k],
                    device(flip_h=True))

    def share_rows(j, core):
        return pl.ds(pl.multiple_of(core * half + j * share, 8), share)

    def ag_copy(k, i, way):
        j = (y - way * i + NY) % NY
        g = (y - way * (i + 1) + NY) % NY
        w = 0 if way > 0 else 1
        return Copy(panel.at[k, share_rows(j, c), :], panel.at[k, share_rows(j, c), :], panel.at[k, share_rows(g, c), :],
                    ag_sem.at[0, k, i, w], ag_sem.at[1, k, i, w], device(dy=way))

    def sib_copy(k, d):
        j = (y - d + NY) % NY
        n = d + 3
        return Copy(panel.at[k, share_rows(j, c), :], panel.at[k, share_rows(j, c), :], panel.at[k, share_rows(j, 1 - c), :],
                    sib_sem.at[0, k, n], sib_sem.at[1, k, n], device(flip_c=True))

    def swapped():
        own_half.wait()
        swap.wait_recv()
        for k in range(sections):
            for way in (1, -1):
                rs_send(k, 0, way)

    events["swap",] = swapped
    steps = {1: NY // 2, -1: NY // 2 - 1}
    for k in range(sections):
        ended = []
        for way in (1, -1):
            for i in range(steps[way]):

                def advance(k=k, i=i, way=way, ended=ended):
                    rs_copy(k, i, way).wait_recv()
                    if i < steps[way] - 1:
                        rs_send(k, i + 1, way)
                    else:
                        ended.append(way)
                    if len(ended) == 2:
                        ended.append(0)
                        ahead = (owner_y[k] - y + NY) % NY
                        mine_out[k] = jnp.where(
                            ahead == 0, stored(k, y), jnp.where(ahead <= 3, left_in[k, 2], right_in[k, 3]))
                        go(cross_copy(k))

                def gathered(k=k, i=i, way=way):
                    ag_copy(k, i, way).wait_recv()
                    if i < steps[way] - 1:
                        go(ag_copy(k, i + 1, way))
                    go(sib_copy(k, way * (i + 1)))

                events["rs", k, i, way] = advance
                events["ag", k, i, way] = gathered

        def crossed(k=k):
            cross_copy(k).wait_recv()
            panel[k, share_rows(y, c), :] = jnp.where(owner_h[k] == h, mine_out[k], other_in[k])
            for way in (1, -1):
                go(ag_copy(k, 0, way))
            go(sib_copy(k, 0))

        events["cross", k] = crossed
        last[k].extend(sib_copy(k, d) for d in range(-3, 5))

    go(swap)
    for k in range(sections):
        for way in (1, -1):
            go(z_copy(k, 1, way))
        for way in (1, -1):
            go(x_copy(k, 0, way))
    for key in ORDER:
        events.pop(key)()
    assert not events
    for k in range(sections):
        for copy in last[k]:
            copy.wait_recv()
        multiply(k, occ_ref, pair_ref, row * (out_ref.shape[0] // TILE), panel, held[k], out_ref)
    for copy in sent:
        copy.wait_send()


def on_device(amplitudes, integrals, owner_column, occ_irrep, pair_irrep):
    tiles_here, slots, tile = amplitudes.shape[1:4]
    sections, _, columns = integrals.shape
    rows = tiles_here * slots * tile
    half, share = rows // NC, rows // NC // NY
    f32 = jnp.float32
    dma = pltpu.SemaphoreType.DMA
    smem = pl.BlockSpec(memory_space=pltpu.SMEM)
    return pl.pallas_call(
        kernel,
        out_shape=jax.ShapeDtypeStruct((tiles_here * tile, columns), f32),
        in_specs=[smem, smem, smem, pl.BlockSpec(memory_space=pl.ANY), pl.BlockSpec(memory_space=pl.ANY)],
        out_specs=pl.BlockSpec(memory_space=pltpu.VMEM),
        scratch_shapes=[
            pltpu.VMEM((NX, NZ, tile, columns), f32),
            pltpu.VMEM((NX, NZ, tile, columns), f32),
            pltpu.VMEM((sections, rows, tile), f32),
            pltpu.VMEM((NC, half, tile), f32),
            pltpu.VMEM((sections, 4, share, tile), f32),
            pltpu.VMEM((sections, 4, share, tile), f32),
            pltpu.VMEM((sections, 3, share, tile), f32),
            pltpu.VMEM((sections, 3, share, tile), f32),
            pltpu.VMEM((sections, share, tile), f32),
            pltpu.VMEM((sections, share, tile), f32),
            dma((1 + sections,)),
            dma((2, sections, 3, 2)),
            dma((2, sections, 4, 4)),
            dma((2, sections, 4)),
            dma((2, sections, 3, 2)),
            dma((2, sections, 4, 2)),
            dma((2, sections, 4, 2)),
            dma((2, sections + 1, 8)),
            dma((2, sections)),
        ],
        compiler_params=pltpu.CompilerParams(
            collective_id=0, has_side_effects=True, vmem_limit_bytes=48 * 1024 * 1024
        ),
        name="ladder",
    )(*(pltpu.with_memory_space_constraint(v, pltpu.HBM)
        for v in (owner_column, occ_irrep, pair_irrep, amplitudes.reshape(rows, tile), integrals)))


def solution(mesh):
    return jax.shard_map(
        on_device,
        mesh=mesh,
        in_specs=(P("col", "row", None, None, None), P(None, "row", "col"), P(), P(), P()),
        out_specs=P("row", "col"),
        check_vma=False,
    )
```

time: 88.3 us -> 81.8 us (0.926); the launches traced: 87.2 us -> 81.7 us
  Pallas kernels: 84.5 us -> 80.5 us
  local copies, waits for them, and re-layouts: 2.67 us -> 1.15 us
    pallas_call x1, Pallas kernels: 84.5 us -> 80.5 us  [on_device(): pl.pallas_call(kernel, out_shape=jax.ShapeDtypeStruct((tiles_here * tile,...]
    unnamed x1, local copies, waits for them, and re-layouts: 2.67 us -> 1.15 us
where the time goes in v3:
time: 81.8 us; the launch traced here: 81.7 us
  Pallas kernels  80.5 us (98%)
  local copies, waits for them, and re-layouts  1.15 us (1%)
    pallas_call x1, Pallas kernels, on_device(): pl.pallas_call(kernel, out_shape=jax.ShapeDtypeStruct((tiles_here * tile,...  80.5 us

profile of v3, /device:TPU:1, one launch (start us, length us, event | category | flops | bytes accessed | tf_op | source)
XLA Modules:
  0.0 81.7 jit_solution(10916575692587976045)
XLA Ops:
  0.0 80.5 %ladder.1 = f32[768,512]{1,0:T(8,128)S(1)} custom-call(s32[2]{0:T(128)} %owner_ref.1, s32[96]{0:T(128)} %occ_ref.1, s32[2,16]{1,0:T(2,128)} %pair_ref.1, f32[3072,128]{1,0:T(8,128)} %bitcast.1, f32[2,128,512]{2,1,0:T(8,128)} %int_ref.1), custom_call_target="tpu_custom_call" | custom-call | tf_op jit(solution)/shard_map/ladder/pallas_call | solution.py:376
  80.5 1.1 %copy.7 = f32[768,512]{1,0:T(8,128)} copy(f32[768,512]{1,0:T(8,128)S(1)} %ladder.1) | data formatting | bytes 3145728

commit v4 on v3

--- a/solution.py
+++ b/solution.py
@@ -13,20 +13,20 @@
 X_ROWS = (24, 16)
 OFFSETS = (0, -1, 1, -2, 2, -3, 3)
 ORDER = (
-    ('fs', 1), ('swap',), ('z', 0, 1, -1), ('fs', 0), ('rs', 0, 0, 1), ('z', 0, 1, 1), ('z', 1, 1, 1),
-    ('rs', 1, 0, 1), ('z', 1, 1, -1), ('rs', 0, 0, -1), ('rs', 1, 0, -1), ('rs', 0, 1, 1), ('rs', 1, 1, 1),
-    ('z', 0, 2, 1), ('f', 0, -1), ('rs', 0, 1, -1), ('rs', 0, 2, 1), ('z', 0, 2, -1), ('rs', 1, 2, 1), ('f', 0, 1),
-    ('f', 1, -1), ('f', 1, 1), ('rs', 1, 1, -1), ('x', 1, 0, 1), ('x', 1, 0, -1), ('rs', 0, 2, -1), ('rs', 0, 3, 1),
-    ('z', 0, 3, 1), ('rs', 1, 3, 1), ('x', 0, 0, 1), ('rs', 1, 2, -1), ('z', 1, 2, 1), ('z', 0, 3, -1),
-    ('z', 1, 2, -1), ('x', 0, 3, -1), ('x', 0, -1, -1), ('x', 0, 1, 1), ('cross', 0), ('fz', 0), ('x', 0, -3, -1),
-    ('x', 0, -3, 1), ('x', 0, 1, -1), ('cross', 1), ('x', 1, 1, 1), ('x', 0, -2, 1), ('z', 1, 3, -1),
-    ('z', 1, 3, 1), ('ag', 0, 0, 1), ('x', 0, 0, -1), ('x', 0, -1, 1), ('x', 0, 2, -1), ('x', 1, -1, 1),
-    ('x', 1, 1, -1), ('fz', 1), ('ag', 1, 0, -1), ('c', 0, 1, -1), ('ag', 1, 0, 1), ('x', 0, -2, -1),
-    ('c', 0, 1, 1), ('x', 1, -1, -1), ('ag', 0, 0, -1), ('ag', 0, 1, 1), ('x', 1, 2, -1), ('c', 1, 1, -1),
-    ('x', 0, 2, 1), ('ag', 1, 1, 1), ('ag', 1, 1, -1), ('x', 1, -2, -1), ('c', 1, 1, 1), ('ag', 0, 2, 1),
-    ('x', 0, 3, 1), ('ag', 0, 1, -1), ('x', 1, 2, 1), ('c', 0, 2, 1), ('c', 0, 2, -1), ('x', 1, -3, 1),
-    ('ag', 1, 2, 1), ('ag', 0, 2, -1), ('c', 1, 2, 1), ('x', 1, -3, -1), ('c', 1, 2, -1), ('x', 1, -2, 1),
-    ('ag', 1, 2, -1), ('x', 1, 3, -1), ('x', 1, 3, 1), ('ag', 0, 3, 1), ('ag', 1, 3, 1),
+    ('swap',), ('fs', 0), ('fs', 1), ('z', 0, 1, -1), ('z', 0, 1, 1), ('rs', 0, 0, 1), ('rs', 1, 0, 1),
+    ('z', 1, 1, 1), ('z', 1, 1, -1), ('rs', 0, 0, -1), ('rs', 1, 0, -1), ('f', 0, -1), ('rs', 0, 1, 1),
+    ('rs', 1, 1, 1), ('z', 0, 2, 1), ('rs', 0, 1, -1), ('z', 0, 2, -1), ('f', 0, 1), ('rs', 0, 2, 1),
+    ('rs', 1, 1, -1), ('rs', 1, 2, 1), ('x', 0, 0, 1), ('rs', 0, 2, -1), ('x', 0, 0, -1), ('f', 1, -1),
+    ('rs', 0, 3, 1), ('z', 0, 3, -1), ('rs', 1, 2, -1), ('f', 1, 1), ('rs', 1, 3, 1), ('x', 1, 0, -1),
+    ('z', 1, 2, -1), ('x', 0, 1, -1), ('z', 1, 2, 1), ('x', 1, 0, 1), ('cross', 0), ('x', 0, 1, 1), ('fz', 0),
+    ('z', 0, 3, 1), ('cross', 1), ('x', 0, -1, -1), ('ag', 0, 0, 1), ('z', 1, 3, 1), ('fz', 1), ('z', 1, 3, -1),
+    ('x', 1, -1, -1), ('x', 0, 2, 1), ('ag', 0, 0, -1), ('x', 0, -2, -1), ('x', 0, 3, 1), ('ag', 1, 0, 1),
+    ('ag', 1, 0, -1), ('x', 0, -1, 1), ('c', 0, 1, -1), ('c', 0, 1, 1), ('x', 0, 2, -1), ('ag', 0, 1, 1),
+    ('x', 1, 1, -1), ('x', 0, -2, 1), ('x', 0, -3, -1), ('ag', 0, 1, -1), ('x', 1, 2, 1), ('ag', 1, 1, 1),
+    ('x', 1, -3, 1), ('x', 1, 1, 1), ('x', 0, -3, 1), ('x', 1, -1, 1), ('ag', 1, 1, -1), ('c', 1, 1, 1),
+    ('x', 1, -3, -1), ('c', 1, 1, -1), ('x', 0, 3, -1), ('ag', 0, 2, 1), ('c', 0, 2, -1), ('c', 0, 2, 1),
+    ('x', 1, 3, -1), ('ag', 1, 2, 1), ('c', 1, 2, 1), ('ag', 0, 2, -1), ('c', 1, 2, -1), ('x', 1, 2, -1),
+    ('ag', 0, 3, 1), ('x', 1, 3, 1), ('x', 1, -2, 1), ('ag', 1, 2, -1), ('x', 1, -2, -1), ('ag', 1, 3, 1),
 )
 
 
@@ -59,18 +59,12 @@
         pl.when(condition)(action)
 
 
-def multiply(k, occ_ref, pair_ref, first, panel, held, out_ref):
-    positions = pair_ref.shape[1]
-    slots = panel.shape[1] // out_ref.shape[0]
-    bf, f32 = jnp.bfloat16, jnp.float32
-
-    def split(value):
-        high = value.astype(bf)
-        return high, (value - high.astype(f32)).astype(bf)
+def find_slots(k, occ_ref, pair_ref, first, index_ref, count_ref):
+    positions, tiles = pair_ref.shape[1], count_ref.shape[0] // pair_ref.shape[0]
+    slots = index_ref.shape[0] // count_ref.shape[0]
 
     def one(o, carry):
         label = occ_ref[first + o]
-        here = pl.ds(pl.multiple_of(o * TILE, TILE), TILE)
         count = jnp.int32(0)
         index = [jnp.int32(0)] * slots
         for t in range(positions):
@@ -78,6 +72,27 @@
             for s in range(min(slots, t + 1)):
                 index[s] = jnp.where(match & (count == s), t, index[s])
             count = count + match.astype(jnp.int32)
+        for s in range(slots):
+            index_ref[(k * tiles + o) * slots + s] = index[s]
+        count_ref[k * tiles + o] = count
+        return carry
+
+    lax.fori_loop(0, tiles, one, 0)
+
+
+def multiply(k, index_ref, count_ref, panel, held, out_ref):
+    tiles = out_ref.shape[0] // TILE
+    slots = panel.shape[1] // out_ref.shape[0]
+    bf, f32 = jnp.bfloat16, jnp.float32
+    dot = functools.partial(jnp.dot, preferred_element_type=f32)
+
+    def split(value):
+        high = value.astype(bf)
+        return high, (value - high.astype(f32)).astype(bf)
+
+    def one(o, carry):
+        here = pl.ds(pl.multiple_of(o * TILE, TILE), TILE)
+        count = count_ref[k * tiles + o]
         total = None if k == 0 else out_ref[here, :]
         for pair in range(slots // 2):
             left, right = [], []
@@ -85,21 +100,23 @@
                 rows = pl.multiple_of((o * slots + s) * TILE, TILE)
                 tile = panel[k, pl.ds(rows, TILE), :]
                 left.append(jnp.where(count > s, tile, 0.0))
-                right.append(held[index[s] // NZ, index[s] % NZ])
+                t = index_ref[(k * tiles + o) * slots + s]
+                right.append(held[t // NZ, t % NZ])
             a_high, a_low = split(jnp.concatenate(left, axis=1))
             b_high, b_low = split(jnp.concatenate(right, axis=0))
-            dot = functools.partial(jnp.dot, preferred_element_type=f32)
-            part = dot(a_high, b_high) + (dot(a_high, b_low) + dot(a_low, b_high))
+            both = dot(jnp.concatenate([a_high, a_low], axis=0), b_high)
+            part = both[:TILE] + (both[TILE:] + dot(a_high, b_low))
             total = part if total is None else total + part
         out_ref[here, :] = total
         return carry
 
-    lax.fori_loop(0, out_ref.shape[0] // TILE, one, 0)
-
-
-def kernel(owner_ref, occ_ref, pair_ref, amp_ref, int_ref, out_ref, held_0, held_1, panel, both, right_out, right_in,
+    lax.fori_loop(0, tiles, one, 0)
+
+
+def kernel(owner_hbm, occ_hbm, pair_hbm, amp_ref, int_ref, out_ref, owner_ref, occ_ref, pair_ref, index_ref, count_ref,
+           held_0, held_1, panel, both, right_out, right_in,
            left_out, left_in, mine_out, other_in, local_sem, z_sem, x_sem, xf_sem, xz_sem, rs_sem, ag_sem, sib_sem,
-           cross_sem):
+           cross_sem, ready_sem):
     row, col = lax.axis_index("row"), lax.axis_index("col")
     x, z = row // NZ, row % NZ
     y, h, c = col // (NH * NC), (col // NC) % NH, col % NC
@@ -120,25 +137,45 @@
         sent.append(copy)
 
     barrier = pltpu.get_barrier_semaphore()
-    partners = [device(dx=1), device(dx=-1), device(dy=1), device(dy=-1), device(flip_h=True), device(flip_c=True)]
-    for partner in partners:
-        pl.semaphore_signal(barrier, inc=1, device_id=partner, device_id_type=MESH)
-
-    @pl.when(z > 0)
-    def _():
-        pl.semaphore_signal(barrier, inc=1, device_id=device(dz=-1), device_id_type=MESH)
-
-    @pl.when(z < NZ - 1)
-    def _():
-        pl.semaphore_signal(barrier, inc=1, device_id=device(dz=1), device_id_type=MESH)
+    greets_up, greets_down, greets_h = y < NY // 2, (y == 0) | (y > NY // 2), h == 0
+    waits_up, waits_down, waits_h = y >= NY // 2, (y > 0) & (y <= NY // 2), h == 1
+
+    def greet(partner, condition=None):
+        guarded(condition, lambda: pl.semaphore_signal(barrier, inc=1, device_id=partner, device_id_type=MESH))
+
+    greet(device(dx=1))
+    greet(device(dx=-1))
+    greet(device(flip_c=True))
+    greet(device(dz=-1), z > 0)
+    greet(device(dz=1), z < NZ - 1)
+    greet(device(dy=1), greets_up)
+    greet(device(dy=-1), greets_down)
+    greet(device(flip_h=True), greets_h)
+    peers = jnp.int32(3)
+    for condition in (z > 0, z < NZ - 1, waits_up, waits_down, waits_h):
+        peers = peers + condition.astype(jnp.int32)
+
+    def answer(n, partner, condition):
+        guarded(condition, lambda: pl.semaphore_signal(
+            ready_sem.at[n], inc=1, device_id=partner, device_id_type=MESH))
+
+    def answered(n, condition):
+        guarded(condition, lambda: pl.semaphore_wait(ready_sem.at[n], 1))
 
     own_ints = [pltpu.make_async_copy(int_ref.at[k], held[k].at[x, z], local_sem.at[1 + k]) for k in range(sections)]
+    labels = [
+        pltpu.make_async_copy(src, dst, local_sem.at[1 + sections + n])
+        for n, (src, dst) in enumerate(((owner_hbm, owner_ref), (occ_hbm, occ_ref), (pair_hbm, pair_ref)))
+    ]
     own_half = pltpu.make_async_copy(
         amp_ref.at[pl.ds(pl.multiple_of(c * half, 8), half), :], both.at[c], local_sem.at[0])
-    for copy in own_ints:
+    for copy in (*labels, *own_ints):
         copy.start()
     own_half.start()
-    pl.semaphore_wait(barrier, len(partners) + (z > 0).astype(jnp.int32) + (z < NZ - 1).astype(jnp.int32))
+    pl.semaphore_wait(barrier, peers)
+    answer(1, device(dy=1), waits_up)
+    answer(0, device(dy=-1), waits_down)
+    answer(2, device(flip_h=True), waits_h)
 
     mid = [(TILE - first) // 16 * 8 for first in X_ROWS]
     zr = [pl.ds(first, TILE - first) for first in X_ROWS]
@@ -260,13 +297,13 @@
     swap = Copy(amp_ref.at[half_rows(1 - c), :], both.at[c], both.at[1 - c], sib_sem.at[0, sections, 0],
                 sib_sem.at[1, sections, 0], device(flip_c=True))
 
-    owner_y = [owner_ref[k] // (NH * NC) for k in range(sections)]
-    owner_h = [(owner_ref[k] // NC) % NH for k in range(sections)]
-    owner_c = [owner_ref[k] % NC for k in range(sections)]
+    def owner(k):
+        col_k = owner_ref[k]
+        return col_k // (NH * NC), (col_k // NC) % NH, col_k % NC
 
     def stored(k, j):
         rows = pl.ds(pl.multiple_of(j * share, 8), share)
-        return jnp.where(owner_c[k] == 0, both[0, rows, :], both[1, rows, :])
+        return jnp.where(owner(k)[2] == 0, both[0, rows, :], both[1, rows, :])
 
     def rs_copy(k, i, way):
         w = 0 if way > 0 else 1
@@ -278,7 +315,7 @@
         src, dst = (right_out, right_in) if way > 0 else (left_out, left_in)
         value = stored(k, j)
         if i:
-            value = jnp.where(owner_y[k] == y, value, dst[k, i - 1])
+            value = jnp.where(owner(k)[0] == y, value, dst[k, i - 1])
         src[k, i] = value
         go(rs_copy(k, i, way))
 
@@ -305,11 +342,14 @@
     def swapped():
         own_half.wait()
         swap.wait_recv()
+        answered(0, greets_up)
+        answered(1, greets_down)
         for k in range(sections):
             for way in (1, -1):
                 rs_send(k, 0, way)
 
     events["swap",] = swapped
+    crossing = []
     steps = {1: NY // 2, -1: NY // 2 - 1}
     for k in range(sections):
         ended = []
@@ -324,9 +364,12 @@
                         ended.append(way)
                     if len(ended) == 2:
                         ended.append(0)
-                        ahead = (owner_y[k] - y + NY) % NY
+                        ahead = (owner(k)[0] - y + NY) % NY
                         mine_out[k] = jnp.where(
                             ahead == 0, stored(k, y), jnp.where(ahead <= 3, left_in[k, 2], right_in[k, 3]))
+                        if not crossing:
+                            crossing.append(k)
+                            answered(2, greets_h)
                         go(cross_copy(k))
 
                 def gathered(k=k, i=i, way=way):
@@ -340,7 +383,7 @@
 
         def crossed(k=k):
             cross_copy(k).wait_recv()
-            panel[k, share_rows(y, c), :] = jnp.where(owner_h[k] == h, mine_out[k], other_in[k])
+            panel[k, share_rows(y, c), :] = jnp.where(owner(k)[1] == h, mine_out[k], other_in[k])
             for way in (1, -1):
                 go(ag_copy(k, 0, way))
             go(sib_copy(k, 0))
@@ -354,15 +397,20 @@
             go(z_copy(k, 1, way))
         for way in (1, -1):
             go(x_copy(k, 0, way))
+    for copy in labels:
+        copy.wait()
+    for k in range(sections):
+        find_slots(k, occ_ref, pair_ref, row * (out_ref.shape[0] // TILE), index_ref, count_ref)
     for key in ORDER:
         events.pop(key)()
     assert not events
     for k in range(sections):
+        if k == sections - 1:
+            for copy in sent:
+                copy.wait_send()
         for copy in last[k]:
             copy.wait_recv()
-        multiply(k, occ_ref, pair_ref, row * (out_ref.shape[0] // TILE), panel, held[k], out_ref)
-    for copy in sent:
-        copy.wait_send()
+        multiply(k, index_ref, count_ref, panel, held[k], out_ref)
 
 
 def on_device(amplitudes, integrals, owner_column, occ_irrep, pair_irrep):
@@ -372,13 +420,18 @@
     half, share = rows // NC, rows // NC // NY
     f32 = jnp.float32
     dma = pltpu.SemaphoreType.DMA
-    smem = pl.BlockSpec(memory_space=pltpu.SMEM)
+    smem = functools.partial(pltpu.SMEM, dtype=jnp.int32)
     return pl.pallas_call(
         kernel,
         out_shape=jax.ShapeDtypeStruct((tiles_here * tile, columns), f32),
-        in_specs=[smem, smem, smem, pl.BlockSpec(memory_space=pl.ANY), pl.BlockSpec(memory_space=pl.ANY)],
+        in_specs=[pl.BlockSpec(memory_space=pl.ANY)] * 5,
         out_specs=pl.BlockSpec(memory_space=pltpu.VMEM),
         scratch_shapes=[
+            smem(owner_column.shape),
+            smem(occ_irrep.shape),
+            smem(pair_irrep.shape),
+            smem((sections * tiles_here * slots,)),
+            smem((sections * tiles_here,)),
             pltpu.VMEM((NX, NZ, tile, columns), f32),
             pltpu.VMEM((NX, NZ, tile, columns), f32),
             pltpu.VMEM((sections, rows, tile), f32),
@@ -389,7 +442,7 @@
             pltpu.VMEM((sections, 3, share, tile), f32),
             pltpu.VMEM((sections, share, tile), f32),
             pltpu.VMEM((sections, share, tile), f32),
-            dma((1 + sections,)),
+            dma((4 + sections,)),
             dma((2, sections, 3, 2)),
             dma((2, sections, 4, 4)),
             dma((2, sections, 4)),
@@ -398,6 +451,7 @@
             dma((2, sections, 4, 2)),
             dma((2, sections + 1, 8)),
             dma((2, sections)),
+            pltpu.SemaphoreType.REGULAR((3,)),
         ],
         compiler_params=pltpu.CompilerParams(
             collective_id=0, has_side_effects=True, vmem_limit_bytes=48 * 1024 * 1024

time: 81.8 us -> 75.8 us (0.927)
  Pallas kernels: 80.5 us -> 74.5 us
    pallas_call x1, Pallas kernels: 80.5 us -> 74.5 us  [on_device(): pl.pallas_call(kernel, out_shape=jax.ShapeDtypeStruct((tiles_here * tile,...]
where the time goes in v4:
time: 75.8 us; the launch traced here: 75.7 us
  Pallas kernels  74.5 us (98%)
  local copies, waits for them, and re-layouts  1.15 us (2%)
    pallas_call x1, Pallas kernels, on_device(): pl.pallas_call(kernel, out_shape=jax.ShapeDtypeStruct((tiles_here * tile,...  74.5 us

profile of v4, /device:TPU:1, one launch (start us, length us, event | category | flops | bytes accessed | tf_op | source)
XLA Modules:
  0.0 75.7 jit_solution(12748675378696526110)
XLA Ops:
  0.0 74.5 %ladder.1 = f32[768,512]{1,0:T(8,128)S(1)} custom-call(s32[2]{0:T(128)} %owner_hbm.1, s32[96]{0:T(128)} %occ_hbm.1, s32[2,16]{1,0:T(2,128)} %pair_hbm.1, f32[3072,128]{1,0:T(8,128)} %bitcast.1, f32[2,128,512]{2,1,0:T(8,128)} %int_ref.1), custom_call_target="tpu_custom_call" | custom-call | tf_op jit(solution)/shard_map/ladder/pallas_call | solution.py:424
  74.5 1.1 %copy.7 = f32[768,512]{1,0:T(8,128)} copy(f32[768,512]{1,0:T(8,128)S(1)} %ladder.1) | data formatting | bytes 3145728

commit v5 on v4

--- a/solution.py
+++ b/solution.py
@@ -10,23 +10,23 @@
 MESH = pl.DeviceIdType.MESH
 NX, NZ, NY, NH, NC = 4, 4, 8, 2, 2
 TILE = 128
-X_ROWS = (24, 16)
+X_ROWS = (24, 24)
 OFFSETS = (0, -1, 1, -2, 2, -3, 3)
 ORDER = (
-    ('swap',), ('fs', 0), ('fs', 1), ('z', 0, 1, -1), ('z', 0, 1, 1), ('rs', 0, 0, 1), ('rs', 1, 0, 1),
-    ('z', 1, 1, 1), ('z', 1, 1, -1), ('rs', 0, 0, -1), ('rs', 1, 0, -1), ('f', 0, -1), ('rs', 0, 1, 1),
-    ('rs', 1, 1, 1), ('z', 0, 2, 1), ('rs', 0, 1, -1), ('z', 0, 2, -1), ('f', 0, 1), ('rs', 0, 2, 1),
-    ('rs', 1, 1, -1), ('rs', 1, 2, 1), ('x', 0, 0, 1), ('rs', 0, 2, -1), ('x', 0, 0, -1), ('f', 1, -1),
-    ('rs', 0, 3, 1), ('z', 0, 3, -1), ('rs', 1, 2, -1), ('f', 1, 1), ('rs', 1, 3, 1), ('x', 1, 0, -1),
-    ('z', 1, 2, -1), ('x', 0, 1, -1), ('z', 1, 2, 1), ('x', 1, 0, 1), ('cross', 0), ('x', 0, 1, 1), ('fz', 0),
-    ('z', 0, 3, 1), ('cross', 1), ('x', 0, -1, -1), ('ag', 0, 0, 1), ('z', 1, 3, 1), ('fz', 1), ('z', 1, 3, -1),
-    ('x', 1, -1, -1), ('x', 0, 2, 1), ('ag', 0, 0, -1), ('x', 0, -2, -1), ('x', 0, 3, 1), ('ag', 1, 0, 1),
-    ('ag', 1, 0, -1), ('x', 0, -1, 1), ('c', 0, 1, -1), ('c', 0, 1, 1), ('x', 0, 2, -1), ('ag', 0, 1, 1),
-    ('x', 1, 1, -1), ('x', 0, -2, 1), ('x', 0, -3, -1), ('ag', 0, 1, -1), ('x', 1, 2, 1), ('ag', 1, 1, 1),
-    ('x', 1, -3, 1), ('x', 1, 1, 1), ('x', 0, -3, 1), ('x', 1, -1, 1), ('ag', 1, 1, -1), ('c', 1, 1, 1),
-    ('x', 1, -3, -1), ('c', 1, 1, -1), ('x', 0, 3, -1), ('ag', 0, 2, 1), ('c', 0, 2, -1), ('c', 0, 2, 1),
-    ('x', 1, 3, -1), ('ag', 1, 2, 1), ('c', 1, 2, 1), ('ag', 0, 2, -1), ('c', 1, 2, -1), ('x', 1, 2, -1),
-    ('ag', 0, 3, 1), ('x', 1, 3, 1), ('x', 1, -2, 1), ('ag', 1, 2, -1), ('x', 1, -2, -1), ('ag', 1, 3, 1),
+    ('swap',), ('fs', 0), ('fs', 1), ('z', 0, 1, 1), ('x', 0, 0, 1), ('z', 0, 1, -1), ('rs', 0, 0, 1),
+    ('rs', 1, 0, 1), ('rs', 0, 0, -1), ('f', 0, -1), ('z', 1, 1, -1), ('z', 1, 1, 1), ('rs', 0, 1, 1),
+    ('rs', 1, 0, -1), ('f', 1, -1), ('f', 0, 1), ('rs', 1, 1, 1), ('f', 1, 1), ('z', 0, 2, 1), ('z', 0, 2, -1),
+    ('rs', 0, 1, -1), ('rs', 0, 2, 1), ('rs', 0, 2, -1), ('rs', 1, 1, -1), ('rs', 1, 2, 1), ('rs', 0, 3, 1),
+    ('x', 0, 0, -1), ('rs', 1, 2, -1), ('rs', 1, 3, 1), ('z', 0, 3, 1), ('x', 0, -1, -1), ('z', 1, 2, 1),
+    ('z', 1, 2, -1), ('x', 0, -3, -1), ('z', 0, 3, -1), ('x', 0, 1, -1), ('x', 0, -1, 1), ('x', 1, 0, 1), ('fz', 0),
+    ('cross', 0), ('x', 0, 2, -1), ('x', 0, 1, 1), ('cross', 1), ('x', 0, 3, 1), ('fz', 1), ('ag', 0, 0, -1),
+    ('ag', 0, 0, 1), ('x', 0, -2, 1), ('z', 1, 3, -1), ('x', 1, 0, -1), ('z', 1, 3, 1), ('c', 0, 1, 1),
+    ('x', 0, 2, 1), ('x', 0, 3, -1), ('c', 0, 1, -1), ('ag', 1, 0, 1), ('ag', 1, 0, -1), ('x', 1, 1, 1),
+    ('x', 1, 2, 1), ('ag', 0, 1, 1), ('x', 0, -2, -1), ('x', 1, -2, -1), ('c', 1, 1, -1), ('c', 1, 1, 1),
+    ('x', 0, -3, 1), ('x', 1, 1, -1), ('ag', 1, 1, 1), ('x', 1, -1, -1), ('ag', 1, 1, -1), ('ag', 0, 1, -1),
+    ('x', 1, -1, 1), ('c', 0, 2, 1), ('c', 0, 2, -1), ('ag', 0, 2, 1), ('x', 1, -3, -1), ('x', 1, 3, -1),
+    ('x', 1, -2, 1), ('ag', 1, 2, 1), ('x', 1, 3, 1), ('c', 1, 2, 1), ('c', 1, 2, -1), ('x', 1, 2, -1),
+    ('ag', 1, 2, -1), ('x', 1, -3, 1), ('ag', 0, 3, 1), ('ag', 0, 2, -1), ('ag', 1, 3, 1),
 )
 
 
@@ -110,7 +110,7 @@
         out_ref[here, :] = total
         return carry
 
-    lax.fori_loop(0, tiles, one, 0)
+    lax.fori_loop(0, tiles, one, 0, unroll=True)
 
 
 def kernel(owner_hbm, occ_hbm, pair_hbm, amp_ref, int_ref, out_ref, owner_ref, occ_ref, pair_ref, index_ref, count_ref,

time: 75.8 us -> 73.3 us (0.967)
  Pallas kernels: 74.5 us -> 71.6 us
    pallas_call x1, Pallas kernels: 74.5 us -> 71.6 us  [on_device(): pl.pallas_call(kernel, out_shape=jax.ShapeDtypeStruct((tiles_here * tile,...]
where the time goes in v5:
time: 73.3 us; the launch traced here: 72.8 us
  Pallas kernels  71.6 us (98%)
  local copies, waits for them, and re-layouts  1.15 us (2%)
    pallas_call x1, Pallas kernels, on_device(): pl.pallas_call(kernel, out_shape=jax.ShapeDtypeStruct((tiles_here * tile,...  71.6 us

profile of v5, /device:TPU:1, one launch (start us, length us, event | category | flops | bytes accessed | tf_op | source)
XLA Modules:
  0.0 72.8 jit_solution(31324068712002855)
XLA Ops:
  0.0 71.6 %ladder.1 = f32[768,512]{1,0:T(8,128)S(1)} custom-call(s32[2]{0:T(128)} %owner_hbm.1, s32[96]{0:T(128)} %occ_hbm.1, s32[2,16]{1,0:T(2,128)} %pair_hbm.1, f32[3072,128]{1,0:T(8,128)} %bitcast.1, f32[2,128,512]{2,1,0:T(8,128)} %int_ref.1), custom_call_target="tpu_custom_call" | custom-call | tf_op jit(solution)/shard_map/ladder/pallas_call | solution.py:424
  71.6 1.1 %copy.7 = f32[768,512]{1,0:T(8,128)} copy(f32[768,512]{1,0:T(8,128)S(1)} %ladder.1) | data formatting | bytes 3145728

commit v6 on v5

--- a/solution.py
+++ b/solution.py
@@ -11,6 +11,7 @@
 NX, NZ, NY, NH, NC = 4, 4, 8, 2, 2
 TILE = 128
 X_ROWS = (24, 24)
+STREAMS = 2
 OFFSETS = (0, -1, 1, -2, 2, -3, 3)
 ORDER = (
     ('swap',), ('fs', 0), ('fs', 1), ('z', 0, 1, 1), ('x', 0, 0, 1), ('z', 0, 1, -1), ('rs', 0, 0, 1),
@@ -116,7 +117,7 @@
 def kernel(owner_hbm, occ_hbm, pair_hbm, amp_ref, int_ref, out_ref, owner_ref, occ_ref, pair_ref, index_ref, count_ref,
            held_0, held_1, panel, both, right_out, right_in,
            left_out, left_in, mine_out, other_in, local_sem, z_sem, x_sem, xf_sem, xz_sem, rs_sem, ag_sem, sib_sem,
-           cross_sem, ready_sem):
+           cross_sem, swap_sem, ready_sem):
     row, col = lax.axis_index("row"), lax.axis_index("col")
     x, z = row // NZ, row % NZ
     y, h, c = col // (NH * NC), (col // NC) % NH, col % NC
@@ -177,7 +178,7 @@
     answer(0, device(dy=-1), waits_down)
     answer(2, device(flip_h=True), waits_h)
 
-    mid = [(TILE - first) // 16 * 8 for first in X_ROWS]
+    mid = [((TILE - first) // 8 + k) // 2 * 8 for k, first in enumerate(X_ROWS)]
     zr = [pl.ds(first, TILE - first) for first in X_ROWS]
     low = [pl.ds(first, m) for first, m in zip(X_ROWS, mid)]
     high = [pl.ds(first + m, TILE - first - m) for first, m in zip(X_ROWS, mid)]
@@ -232,7 +233,7 @@
                 events["x", k, d, way] = passed
                 last[k].append(x_forward(k, d, way))
 
-    cut = [first // 16 * 8 for first in X_ROWS]
+    cut = [(first // 8 + k) // 2 * 8 for k, first in enumerate(X_ROWS)]
     xr = [pl.ds(0, first) for first in X_ROWS]
     xlow = [pl.ds(0, m) for m in cut]
     xhigh = [pl.ds(m, first - m) for first, m in zip(X_ROWS, cut)]
@@ -294,104 +295,122 @@
     def half_rows(core):
         return pl.ds(pl.multiple_of(core * half, 8), half)
 
-    swap = Copy(amp_ref.at[half_rows(1 - c), :], both.at[c], both.at[1 - c], sib_sem.at[0, sections, 0],
-                sib_sem.at[1, sections, 0], device(flip_c=True))
+    def swap_copy(n):
+        j = (y + NY // 2 + (-(n // 2) if n % 2 == 0 else n // 2 + 1)) % NY
+
+        def rows_of(core):
+            return pl.ds(pl.multiple_of(core * half + j * share, 8), share)
+
+        part = pl.ds(pl.multiple_of(j * share, 8), share)
+        return Copy(amp_ref.at[rows_of(1 - c), :], both.at[c, part, :], both.at[1 - c, part, :],
+                    swap_sem.at[0, n], swap_sem.at[1, n], device(flip_c=True))
 
     def owner(k):
         col_k = owner_ref[k]
         return col_k // (NH * NC), (col_k // NC) % NH, col_k % NC
 
-    def stored(k, j):
-        rows = pl.ds(pl.multiple_of(j * share, 8), share)
-        return jnp.where(owner(k)[2] == 0, both[0, rows, :], both[1, rows, :])
-
-    def rs_copy(k, i, way):
+    pieces = STREAMS // sections
+    piece = share // pieces
+    have = set()
+
+    def need(n):
+        if n not in have:
+            have.add(n)
+            swap_copy(n).wait_recv()
+
+    def stored(q, j):
+        rows = pl.ds(pl.multiple_of(j * share + q % pieces * piece, 8), piece)
+        return jnp.where(owner(q // pieces)[2] == 0, both[0, rows, :], both[1, rows, :])
+
+    def rs_copy(q, i, way):
         w = 0 if way > 0 else 1
         src, dst = (right_out, right_in) if way > 0 else (left_out, left_in)
-        return Copy(src.at[k, i], dst.at[k, i], dst.at[k, i], rs_sem.at[0, k, i, w], rs_sem.at[1, k, i, w], device(dy=way))
-
-    def rs_send(k, i, way):
+        return Copy(src.at[q, i], dst.at[q, i], dst.at[q, i], rs_sem.at[0, q, i, w], rs_sem.at[1, q, i, w], device(dy=way))
+
+    def rs_send(q, i, way):
         j = (y + 4 - i) % NY if way > 0 else (y - 3 + i + NY) % NY
         src, dst = (right_out, right_in) if way > 0 else (left_out, left_in)
-        value = stored(k, j)
+        need(2 * i + (way < 0))
+        value = stored(q, j)
         if i:
-            value = jnp.where(owner(k)[0] == y, value, dst[k, i - 1])
-        src[k, i] = value
-        go(rs_copy(k, i, way))
-
-    def cross_copy(k):
-        return Copy(mine_out.at[k], other_in.at[k], other_in.at[k], cross_sem.at[0, k], cross_sem.at[1, k],
+            value = jnp.where(owner(q // pieces)[0] == y, value, dst[q, i - 1])
+        src[q, i] = value
+        go(rs_copy(q, i, way))
+
+    def cross_copy(q):
+        return Copy(mine_out.at[q], other_in.at[q], other_in.at[q], cross_sem.at[0, q], cross_sem.at[1, q],
                     device(flip_h=True))
 
-    def share_rows(j, core):
-        return pl.ds(pl.multiple_of(core * half + j * share, 8), share)
-
-    def ag_copy(k, i, way):
+    def share_rows(q, j, core):
+        return pl.ds(pl.multiple_of(core * half + j * share + q % pieces * piece, 8), piece)
+
+    def ag_copy(q, i, way):
         j = (y - way * i + NY) % NY
         g = (y - way * (i + 1) + NY) % NY
         w = 0 if way > 0 else 1
-        return Copy(panel.at[k, share_rows(j, c), :], panel.at[k, share_rows(j, c), :], panel.at[k, share_rows(g, c), :],
-                    ag_sem.at[0, k, i, w], ag_sem.at[1, k, i, w], device(dy=way))
-
-    def sib_copy(k, d):
+        return Copy(panel.at[q // pieces, share_rows(q, j, c), :], panel.at[q // pieces, share_rows(q, j, c), :], panel.at[q // pieces, share_rows(q, g, c), :],
+                    ag_sem.at[0, q, i, w], ag_sem.at[1, q, i, w], device(dy=way))
+
+    def sib_copy(q, d):
         j = (y - d + NY) % NY
         n = d + 3
-        return Copy(panel.at[k, share_rows(j, c), :], panel.at[k, share_rows(j, c), :], panel.at[k, share_rows(j, 1 - c), :],
-                    sib_sem.at[0, k, n], sib_sem.at[1, k, n], device(flip_c=True))
+        return Copy(panel.at[q // pieces, share_rows(q, j, c), :], panel.at[q // pieces, share_rows(q, j, c), :], panel.at[q // pieces, share_rows(q, j, 1 - c), :],
+                    sib_sem.at[0, q, n], sib_sem.at[1, q, n], device(flip_c=True))
 
     def swapped():
         own_half.wait()
-        swap.wait_recv()
         answered(0, greets_up)
         answered(1, greets_down)
-        for k in range(sections):
-            for way in (1, -1):
-                rs_send(k, 0, way)
+        for q in range(STREAMS):
+            for way in (1, -1):
+                rs_send(q, 0, way)
 
     events["swap",] = swapped
     crossing = []
     steps = {1: NY // 2, -1: NY // 2 - 1}
-    for k in range(sections):
+    for q in range(STREAMS):
         ended = []
         for way in (1, -1):
             for i in range(steps[way]):
 
-                def advance(k=k, i=i, way=way, ended=ended):
-                    rs_copy(k, i, way).wait_recv()
+                def advance(q=q, i=i, way=way, ended=ended):
+                    rs_copy(q, i, way).wait_recv()
                     if i < steps[way] - 1:
-                        rs_send(k, i + 1, way)
+                        rs_send(q, i + 1, way)
                     else:
                         ended.append(way)
                     if len(ended) == 2:
                         ended.append(0)
-                        ahead = (owner(k)[0] - y + NY) % NY
-                        mine_out[k] = jnp.where(
-                            ahead == 0, stored(k, y), jnp.where(ahead <= 3, left_in[k, 2], right_in[k, 3]))
+                        need(NY - 1)
+                        ahead = (owner(q // pieces)[0] - y + NY) % NY
+                        mine_out[q] = jnp.where(
+                            ahead == 0, stored(q, y), jnp.where(ahead <= 3, left_in[q, 2], right_in[q, 3]))
                         if not crossing:
-                            crossing.append(k)
+                            crossing.append(q)
                             answered(2, greets_h)
-                        go(cross_copy(k))
-
-                def gathered(k=k, i=i, way=way):
-                    ag_copy(k, i, way).wait_recv()
+                        go(cross_copy(q))
+
+                def gathered(q=q, i=i, way=way):
+                    ag_copy(q, i, way).wait_recv()
                     if i < steps[way] - 1:
-                        go(ag_copy(k, i + 1, way))
-                    go(sib_copy(k, way * (i + 1)))
-
-                events["rs", k, i, way] = advance
-                events["ag", k, i, way] = gathered
-
-        def crossed(k=k):
-            cross_copy(k).wait_recv()
-            panel[k, share_rows(y, c), :] = jnp.where(owner(k)[1] == h, mine_out[k], other_in[k])
-            for way in (1, -1):
-                go(ag_copy(k, 0, way))
-            go(sib_copy(k, 0))
-
-        events["cross", k] = crossed
-        last[k].extend(sib_copy(k, d) for d in range(-3, 5))
-
-    go(swap)
+                        go(ag_copy(q, i + 1, way))
+                    go(sib_copy(q, way * (i + 1)))
+
+                events["rs", q, i, way] = advance
+                events["ag", q, i, way] = gathered
+
+        def crossed(q=q):
+            cross_copy(q).wait_recv()
+            panel[q // pieces, share_rows(q, y, c), :] = jnp.where(owner(q // pieces)[1] == h, mine_out[q], other_in[q])
+            for way in (1, -1):
+                go(ag_copy(q, 0, way))
+            go(sib_copy(q, 0))
+
+        events["cross", q] = crossed
+        last[q // pieces].extend(sib_copy(q, d) for d in range(-3, 5))
+
+    for n in range(NY):
+        go(swap_copy(n))
     for k in range(sections):
         for way in (1, -1):
             go(z_copy(k, 1, way))
@@ -418,6 +437,7 @@
     sections, _, columns = integrals.shape
     rows = tiles_here * slots * tile
     half, share = rows // NC, rows // NC // NY
+    piece = share * sections // STREAMS
     f32 = jnp.float32
     dma = pltpu.SemaphoreType.DMA
     smem = functools.partial(pltpu.SMEM, dtype=jnp.int32)
@@ -436,21 +456,22 @@
             pltpu.VMEM((NX, NZ, tile, columns), f32),
             pltpu.VMEM((sections, rows, tile), f32),
             pltpu.VMEM((NC, half, tile), f32),
-            pltpu.VMEM((sections, 4, share, tile), f32),
-            pltpu.VMEM((sections, 4, share, tile), f32),
-            pltpu.VMEM((sections, 3, share, tile), f32),
-            pltpu.VMEM((sections, 3, share, tile), f32),
-            pltpu.VMEM((sections, share, tile), f32),
-            pltpu.VMEM((sections, share, tile), f32),
+            pltpu.VMEM((STREAMS, 4, piece, tile), f32),
+            pltpu.VMEM((STREAMS, 4, piece, tile), f32),
+            pltpu.VMEM((STREAMS, 3, piece, tile), f32),
+            pltpu.VMEM((STREAMS, 3, piece, tile), f32),
+            pltpu.VMEM((STREAMS, piece, tile), f32),
+            pltpu.VMEM((STREAMS, piece, tile), f32),
             dma((4 + sections,)),
             dma((2, sections, 3, 2)),
             dma((2, sections, 4, 4)),
             dma((2, sections, 4)),
             dma((2, sections, 3, 2)),
-            dma((2, sections, 4, 2)),
-            dma((2, sections, 4, 2)),
-            dma((2, sections + 1, 8)),
-            dma((2, sections)),
+            dma((2, STREAMS, 4, 2)),
+            dma((2, STREAMS, 4, 2)),
+            dma((2, STREAMS, 8)),
+            dma((2, STREAMS)),
+            dma((2, NY)),
             pltpu.SemaphoreType.REGULAR((3,)),
         ],
         compiler_params=pltpu.CompilerParams(

time: 73.3 us -> 73.3 us (level)
  no operation moved by 1% of the time
where the time goes in v6:
time: 73.3 us; the launch traced here: 72.1 us
  Pallas kernels  70.9 us (97%)
  local copies, waits for them, and re-layouts  1.15 us (2%)
    pallas_call x1, Pallas kernels, on_device(): pl.pallas_call(kernel, out_shape=jax.ShapeDtypeStruct((tiles_here * tile,...  70.9 us

profile of v6, /device:TPU:1, one launch (start us, length us, event | category | flops | bytes accessed | tf_op | source)
XLA Modules:
  0.0 72.1 jit_solution(5752507395083262364)
XLA Ops:
  0.0 70.9 %ladder.1 = f32[768,512]{1,0:T(8,128)S(1)} custom-call(s32[2]{0:T(128)} %owner_hbm.1, s32[96]{0:T(128)} %occ_hbm.1, s32[2,16]{1,0:T(2,128)} %pair_hbm.1, f32[3072,128]{1,0:T(8,128)} %bitcast.1, f32[2,128,512]{2,1,0:T(8,128)} %int_ref.1), custom_call_target="tpu_custom_call" | custom-call | tf_op jit(solution)/shard_map/ladder/pallas_call | solution.py:444
  70.9 1.1 %copy.7 = f32[768,512]{1,0:T(8,128)} copy(f32[768,512]{1,0:T(8,128)S(1)} %ladder.1) | data formatting | bytes 3145728

commit v7 on v6

--- a/solution.py
+++ b/solution.py
@@ -14,7 +14,7 @@
 STREAMS = 2
 OFFSETS = (0, -1, 1, -2, 2, -3, 3)
 ORDER = (
-    ('swap',), ('fs', 0), ('fs', 1), ('z', 0, 1, 1), ('x', 0, 0, 1), ('z', 0, 1, -1), ('rs', 0, 0, 1),
+    ('fs', 0), ('fs', 1), ('swap',), ('z', 0, 1, 1), ('x', 0, 0, 1), ('z', 0, 1, -1), ('rs', 0, 0, 1),
     ('rs', 1, 0, 1), ('rs', 0, 0, -1), ('f', 0, -1), ('z', 1, 1, -1), ('z', 1, 1, 1), ('rs', 0, 1, 1),
     ('rs', 1, 0, -1), ('f', 1, -1), ('f', 0, 1), ('rs', 1, 1, 1), ('f', 1, 1), ('z', 0, 2, 1), ('z', 0, 2, -1),
     ('rs', 0, 1, -1), ('rs', 0, 2, 1), ('rs', 0, 2, -1), ('rs', 1, 1, -1), ('rs', 1, 2, 1), ('rs', 0, 3, 1),
@@ -291,9 +291,6 @@
                 go(fz_copy(k, 1, way))
 
         events["fz", k] = far
-
-    def half_rows(core):
-        return pl.ds(pl.multiple_of(core * half, 8), half)
 
     def swap_copy(n):
         j = (y + NY // 2 + (-(n // 2) if n % 2 == 0 else n // 2 + 1)) % NY

time: 73.3 us -> 73.3 us (level)
  no operation moved by 1% of the time
where the time goes in v7:
time: 73.3 us; the launch traced here: 72.1 us
  Pallas kernels  70.9 us (97%)
  local copies, waits for them, and re-layouts  1.15 us (2%)
    pallas_call x1, Pallas kernels, on_device(): pl.pallas_call(kernel, out_shape=jax.ShapeDtypeStruct((tiles_here * tile,...  70.9 us

profile of v7, /device:TPU:1, one launch (start us, length us, event | category | flops | bytes accessed | tf_op | source)
XLA Modules:
  0.0 72.1 jit_solution(7310805519932537251)
XLA Ops:
  0.0 70.9 %ladder.1 = f32[768,512]{1,0:T(8,128)S(1)} custom-call(s32[2]{0:T(128)} %owner_hbm.1, s32[96]{0:T(128)} %occ_hbm.1, s32[2,16]{1,0:T(2,128)} %pair_hbm.1, f32[3072,128]{1,0:T(8,128)} %bitcast.1, f32[2,128,512]{2,1,0:T(8,128)} %int_ref.1), custom_call_target="tpu_custom_call" | custom-call | tf_op jit(solution)/shard_map/ladder/pallas_call | solution.py:441
  70.9 1.1 %copy.7 = f32[768,512]{1,0:T(8,128)} copy(f32[768,512]{1,0:T(8,128)S(1)} %ladder.1) | data formatting | bytes 3145728
